TPU v7x, 32 devices: a whole 2x2x4 slice. The times are simulated.
32 devices in a mesh: dp: 8 (over y, x, core), tensor: 4 (over z).
Axes of the slice: x: 2, y: 2, z: 4, core: 2. Of those that a mesh axis runs over, the one named last changes fastest.
Arguments:
- inputs: bfloat16 [8192, 1536], P(('dp', 'tensor')), may hold values from -12 to 12
- norm1_gain: float32 [1536], replicated, may hold values from 0.5 to 1.5
- w_in_x: bfloat16 [1536, 2048], P('dp', 'tensor'), may hold values from -0.15625 to 0.15625
- w_in_y: bfloat16 [1536, 2048], P('dp', 'tensor'), may hold values from -0.15625 to 0.15625
- conv_w: float32 [4, 2048], P(None, 'tensor'), may hold values from -3 to 3
- conv_b: float32 [2048], P('tensor'), may hold values from -1.8 to 1.8
- gates: bfloat16 [2, 16, 128, 128], P(None, 'tensor', 'dp'), may hold values from -0.5 to 0.5
- gate_bias: float32 [2, 2048], P(None, 'tensor'), may hold values from -1 to 1
- decay_param: float32 [2048], P('tensor'), may hold values from -7 to -1
- w_out: bfloat16 [1536, 2048], P('dp', 'tensor'), may hold values from -0.375 to 0.375
- norm2_gain: float32 [1536], replicated, may hold values from 0.5 to 1.5
- w_gate: bfloat16 [1536, 4608], P('dp', 'tensor'), may hold values from -0.15625 to 0.15625
- w_up: bfloat16 [1536, 4608], P('dp', 'tensor'), may hold values from -0.15625 to 0.15625
- w_down: bfloat16 [1536, 4608], P('dp', 'tensor'), may hold values from -0.125 to 0.125
- cotangent: bfloat16 [8192, 1536], P(('dp', 'tensor')), may hold values from -6 to 6
Outputs:
- output: bfloat16 [8192, 1536], P(('dp', 'tensor'))
- grad_inputs: bfloat16 [8192, 1536], P(('dp', 'tensor'))
- grad_norm1_gain: float32 [1536], replicated
- grad_w_in_x: float32 [1536, 2048], P('dp', 'tensor')
- grad_w_in_y: float32 [1536, 2048], P('dp', 'tensor')
- grad_conv_w: float32 [4, 2048], replicated
- grad_conv_b: float32 [2048], replicated
- grad_gates: float32 [2, 16, 128, 128], P(None, 'tensor', 'dp')
- grad_gate_bias: float32 [2, 2048], replicated
- grad_decay_param: float32 [2048], replicated
- grad_w_out: float32 [1536, 2048], P('dp', 'tensor')
- grad_norm2_gain: float32 [1536], replicated
- grad_w_gate: float32 [1536, 4608], P('dp', 'tensor')
- grad_w_up: float32 [1536, 4608], P('dp', 'tensor')
- grad_w_down: float32 [1536, 4608], P('dp', 'tensor')
- stream_rms: float32 [4], replicated
All inputs are finite; a program needn't handle non-finite values.
Results may differ from a plain program's by a relative error of at most 0.0085.
Values may be sent and summed in bfloat16 or wider, within the bound.
A program may use at most 192 MiB of HBM per device.

v0:
```python
import jax
import jax.numpy as jnp
from jax import lax
from jax.sharding import PartitionSpec as P

CONV = 4
SEQ_LEN = 1024


epsilon = 1e-06


def gelu_tanh(value):
    return jax.nn.gelu(value, approximate=True)


def combine(earlier, later):
    return (earlier[0] * later[0], later[0] * earlier[1] + later[1])


def norm_back(value, scale, gain, grad):
    scaled = gain * grad
    return scale * scaled - value * scale * scale * scale * jnp.mean(
        scaled * value, axis=1, keepdims=True
    )


def row_product(left, right):
    return lax.dot_general(
        left, right, (((0,), (0,)), ((), ())), preferred_element_type=jnp.float32
    )


def back_product(left, right):
    return lax.dot_general(
        left, right, (((1,), (1,)), ((), ())), preferred_element_type=jnp.float32
    )


def local(
    inputs,
    norm1_gain,
    w_in_x,
    w_in_y,
    conv_w,
    conv_b,
    gates,
    gate_bias,
    decay_param,
    w_out,
    norm2_gain,
    w_gate,
    w_up,
    w_down,
    cotangent,
):
    row_count = inputs.shape[0]
    model_width = inputs.shape[1]
    tensor_count = lax.axis_size("tensor")
    group_rows = row_count * tensor_count
    seq_count = group_rows // SEQ_LEN
    rec_x, rec_y, rec_o, gate_mats = (
        lax.all_gather(w_in_x, "dp", axis=0, tiled=True),
        lax.all_gather(w_in_y, "dp", axis=0, tiled=True),
        lax.all_gather(w_out, "dp", axis=0, tiled=True),
        lax.all_gather(gates, "dp", axis=2, tiled=True),
    )
    channels = rec_x.shape[1]
    blocks_here = gate_mats.shape[1]
    block_width = gate_mats.shape[3]
    residual = inputs.astype(jnp.float32)
    scale_one = lax.rsqrt(jnp.mean(residual * residual, axis=1, keepdims=True) + epsilon)
    n_one = (residual * scale_one * norm1_gain).astype(jnp.bfloat16)
    full_one = lax.all_gather(n_one, "tensor", axis=0, tiled=True)
    x_branch = jnp.dot(full_one, rec_x, preferred_element_type=jnp.float32)
    y_pre = jnp.dot(full_one, rec_y, preferred_element_type=jnp.float32)
    seq_x = x_branch.reshape(seq_count, SEQ_LEN, channels)
    padded = jnp.pad(seq_x, ((0, 0), (CONV - 1, 0), (0, 0)))
    conv_sum = conv_b + jnp.zeros_like(seq_x)
    for k in range(CONV):
        conv_sum = conv_sum + conv_w[k] * padded[:, CONV - 1 - k : CONV - 1 - k + SEQ_LEN]
    conv_low = conv_sum.reshape(group_rows, channels).astype(jnp.bfloat16)
    conv_value = conv_low.astype(jnp.float32)
    blocked = conv_low.reshape(group_rows, blocks_here, block_width)
    z_input = (
        jnp.einsum(
            "gbi,bij->gbj", blocked, gate_mats[0], preferred_element_type=jnp.float32
        ).reshape(group_rows, channels)
        + gate_bias[0]
    )
    z_decay = (
        jnp.einsum(
            "gbi,bij->gbj", blocked, gate_mats[1], preferred_element_type=jnp.float32
        ).reshape(group_rows, channels)
        + gate_bias[1]
    )
    seq_start = (jnp.arange(group_rows) % SEQ_LEN == 0)[:, None]

    def coefficients(input_pre, decay_pre, conv_part, decay_raw):
        log_decay = -8.0 * jax.nn.sigmoid(decay_pre) * jax.nn.softplus(decay_raw)
        mult = jnp.where(seq_start, 1.0, jnp.sqrt(-jnp.expm1(2.0 * log_decay)))
        return (jnp.exp(log_decay), mult * jax.nn.sigmoid(input_pre) * conv_part)

    (decays, inflow), pull_coeff = jax.vjp(coefficients, z_input, z_decay, conv_value, decay_param)
    seq_decay = decays.reshape(seq_count, SEQ_LEN, channels)
    _, seq_states = lax.associative_scan(
        combine, (seq_decay, inflow.reshape(seq_count, SEQ_LEN, channels)), axis=1
    )
    states = seq_states.reshape(group_rows, channels)
    y_gate = gelu_tanh(y_pre)
    mixed_out = (states * y_gate).astype(jnp.bfloat16)
    branch = lax.psum_scatter(
        back_product(mixed_out, rec_o), "tensor", scatter_dimension=0, tiled=True
    )
    stream = residual + branch
    mlp_g, mlp_u, mlp_d = (
        lax.all_gather(w_gate, "dp", axis=0, tiled=True),
        lax.all_gather(w_up, "dp", axis=0, tiled=True),
        lax.all_gather(w_down, "dp", axis=0, tiled=True),
    )
    scale_two = lax.rsqrt(jnp.mean(stream * stream, axis=1, keepdims=True) + epsilon)
    n_two = (stream * scale_two * norm2_gain).astype(jnp.bfloat16)
    full_two = lax.all_gather(n_two, "tensor", axis=0, tiled=True)
    gate_pre = jnp.dot(full_two, mlp_g, preferred_element_type=jnp.float32)
    up_pre = jnp.dot(full_two, mlp_u, preferred_element_type=jnp.float32)
    hidden = (gelu_tanh(gate_pre) * up_pre).astype(jnp.bfloat16)
    ffn_out = lax.psum_scatter(
        back_product(hidden, mlp_d), "tensor", scatter_dimension=0, tiled=True
    )
    result = stream + ffn_out
    output = result.astype(jnp.bfloat16)
    squares = jnp.stack(
        [
            jnp.sum(stream * stream),
            jnp.sum(branch * branch),
            jnp.sum(ffn_out * ffn_out),
            jnp.sum(result * result),
        ]
    )
    upstream = cotangent.astype(jnp.float32)
    full_cot = lax.all_gather(cotangent, "tensor", axis=0, tiled=True)
    d_hidden = jnp.dot(full_cot, mlp_d, preferred_element_type=jnp.float32)
    grad_down = row_product(full_cot, hidden)
    _, pull_mlp = jax.vjp(
        lambda gate_value, up_value: gelu_tanh(gate_value) * up_value, gate_pre, up_pre
    )
    d_gate, d_up = pull_mlp(d_hidden)
    d_gate_low = d_gate.astype(jnp.bfloat16)
    d_up_low = d_up.astype(jnp.bfloat16)
    grad_gate_w = row_product(full_two, d_gate_low)
    grad_up_w = row_product(full_two, d_up_low)
    d_two = lax.psum_scatter(
        back_product(d_gate_low, mlp_g) + back_product(d_up_low, mlp_u),
        "tensor",
        scatter_dimension=0,
        tiled=True,
    )
    grad_gain_two = jnp.sum(d_two * stream * scale_two, axis=0)
    d_stream = upstream + norm_back(stream, scale_two, norm2_gain, d_two)
    mlp_summed = (grad_gate_w, grad_up_w, grad_down)
    full_branch = lax.all_gather(d_stream.astype(jnp.bfloat16), "tensor", axis=0, tiled=True)
    d_mixed = jnp.dot(full_branch, rec_o, preferred_element_type=jnp.float32)
    grad_out_w = row_product(full_branch, mixed_out)
    d_states = d_mixed * y_gate
    _, pull_gelu = jax.vjp(gelu_tanh, y_pre)
    d_y_low = pull_gelu(d_mixed * states)[0].astype(jnp.bfloat16)
    next_decay = jnp.concatenate([seq_decay[:, 1:], jnp.zeros_like(seq_decay[:, :1])], axis=1)
    _, carried = lax.associative_scan(
        combine, (next_decay, d_states.reshape(seq_count, SEQ_LEN, channels)), reverse=True, axis=1
    )
    prev_states = jnp.concatenate([jnp.zeros_like(seq_states[:, :1]), seq_states[:, :-1]], axis=1)
    d_decays = (carried * prev_states).reshape(group_rows, channels)
    d_input_pre, d_decay_pre, d_conv_direct, grad_decay = pull_coeff(
        (d_decays, carried.reshape(group_rows, channels))
    )
    d_input_low = d_input_pre.astype(jnp.bfloat16)
    d_decay_low = d_decay_pre.astype(jnp.bfloat16)
    grad_bias = jnp.stack(
        [
            jnp.sum(d_input_low, axis=0, dtype=jnp.float32),
            jnp.sum(d_decay_low, axis=0, dtype=jnp.float32),
        ]
    )
    input_blocks = d_input_low.reshape(group_rows, blocks_here, block_width)
    decay_blocks = d_decay_low.reshape(group_rows, blocks_here, block_width)
    grad_gate_mats = jnp.stack(
        [
            jnp.einsum("gbi,gbj->bij", blocked, input_blocks, preferred_element_type=jnp.float32),
            jnp.einsum("gbi,gbj->bij", blocked, decay_blocks, preferred_element_type=jnp.float32),
        ]
    )
    d_conv = d_conv_direct + jnp.einsum(
        "gbj,bij->gbi", input_blocks, gate_mats[0], preferred_element_type=jnp.float32
    ).reshape(group_rows, channels)
    d_conv = d_conv + jnp.einsum(
        "gbj,bij->gbi", decay_blocks, gate_mats[1], preferred_element_type=jnp.float32
    ).reshape(group_rows, channels)
    seq_dconv = d_conv.reshape(seq_count, SEQ_LEN, channels)
    grad_conv_b = jnp.sum(seq_dconv, axis=(0, 1))
    padded_back = jnp.pad(seq_dconv, ((0, 0), (0, CONV - 1), (0, 0)))
    tap_grads = []
    d_x_seq = jnp.zeros_like(seq_dconv)
    for k in range(CONV):
        tap_grads.append(
            jnp.sum(seq_dconv * padded[:, CONV - 1 - k : CONV - 1 - k + SEQ_LEN], axis=(0, 1))
        )
        d_x_seq = d_x_seq + conv_w[k] * padded_back[:, k : k + SEQ_LEN]
    grad_conv_w = jnp.stack(tap_grads)
    d_x_low = d_x_seq.reshape(group_rows, channels).astype(jnp.bfloat16)
    grad_in_x_w = row_product(full_one, d_x_low)
    grad_in_y_w = row_product(full_one, d_y_low)
    d_one = lax.psum_scatter(
        back_product(d_x_low, rec_x) + back_product(d_y_low, rec_y),
        "tensor",
        scatter_dimension=0,
        tiled=True,
    )
    grad_gain_one = jnp.sum(d_one * residual * scale_one, axis=0)
    grad_inputs = (d_stream + norm_back(residual, scale_one, norm1_gain, d_one)).astype(
        jnp.bfloat16
    )
    small_grads = jnp.concatenate(
        [grad_conv_w, grad_conv_b[None], grad_bias, grad_decay[None]], axis=0
    )
    spread_grads = lax.dynamic_update_slice(
        jnp.zeros((small_grads.shape[0], channels * tensor_count), jnp.float32),
        small_grads,
        (0, lax.axis_index("tensor") * channels),
    )
    gain_total, small_total, square_total = lax.psum(
        (jnp.stack([grad_gain_one, grad_gain_two]), spread_grads, squares), ("dp", "tensor")
    )
    stream_rms = jnp.sqrt(
        square_total / (row_count * lax.axis_size("dp") * tensor_count * model_width)
    )
    summed_all = (
        lax.psum_scatter(grad_in_x_w, "dp", scatter_dimension=0, tiled=True),
        lax.psum_scatter(grad_in_y_w, "dp", scatter_dimension=0, tiled=True),
        lax.psum_scatter(grad_out_w, "dp", scatter_dimension=0, tiled=True),
        lax.psum_scatter(grad_gate_mats, "dp", scatter_dimension=2, tiled=True),
        lax.psum_scatter(mlp_summed[0], "dp", scatter_dimension=0, tiled=True),
        lax.psum_scatter(mlp_summed[1], "dp", scatter_dimension=0, tiled=True),
        lax.psum_scatter(mlp_summed[2], "dp", scatter_dimension=0, tiled=True),
    )
    rec_summed = summed_all[:4]
    grad_gate_sum, grad_up_sum, grad_down_sum = (summed_all[4], summed_all[5], summed_all[6])
    return (
        output,
        grad_inputs,
        gain_total[0],
        rec_summed[0],
        rec_summed[1],
        small_total[0:CONV],
        small_total[CONV],
        rec_summed[3],
        small_total[CONV + 1 : CONV + 3],
        small_total[CONV + 3],
        rec_summed[2],
        gain_total[1],
        grad_gate_sum,
        grad_up_sum,
        grad_down_sum,
        stream_rms,
    )


def solution(mesh):
    return jax.shard_map(
        local,
        mesh=mesh,
        in_specs=(
            P(("dp", "tensor"), None),
            P(),
            P("dp", "tensor"),
            P("dp", "tensor"),
            P(None, "tensor"),
            P("tensor"),
            P(None, "tensor", "dp", None),
            P(None, "tensor"),
            P("tensor"),
            P("dp", "tensor"),
            P(),
            P("dp", "tensor"),
            P("dp", "tensor"),
            P("dp", "tensor"),
            P(("dp", "tensor"), None),
        ),
        out_specs=(
            P(("dp", "tensor"), None),
            P(("dp", "tensor"), None),
            P(),
            P("dp", "tensor"),
            P("dp", "tensor"),
            P(),
            P(),
            P(None, "tensor", "dp", None),
            P(),
            P(),
            P("dp", "tensor"),
            P(),
            P("dp", "tensor"),
            P("dp", "tensor"),
            P("dp", "tensor"),
            P(),
        ),
        check_vma=False,
    )
```

profile of v0, /device:TPU:4, one launch (start us, length us, event | category | flops | bytes accessed | tf_op | source)
XLA Modules:
  0.0 1920.8 jit_solution(16737749595569484958)
XLA Ops:
  13.7 9.8 all_gather.35
  24.5 12.7 all-gather.13.cloned.1.call-done
  37.2 65.7 %all-gather.11.cloned.1.call-done = bf16[1024,1536]{1,0:T(8,128)(2,1)} async-done(((bf16[256,1536]{1,0:T(8,128)(2,1)}), bf16[1024,1536]{1,0:T(8,128)(2,1)}) %all-gather.11.cloned.1.call-update) | async-done | bytes 3145744 | tf_op jit(solution)/shard_map/all_gather | solution.py:74
  123.3 6.3 slice.563
  256.7 6.4 slice.561
  263.1 6.3 slice.634
  305.8 8.6 pad.152
  318.2 8.7 pad.151
  326.9 7.5 fusion.34
  341.3 108.7 %reduce-scatter.14.cloned.1.call-done = f32[256,1536]{1,0:T(8,128)} async-done(((f32[1024,1536]{1,0:T(8,128)}), f32[256,1536]{1,0:T(8,128)}) %reduce-scatter.14.cloned.1.call-update) | async-done | bytes 1572880 | tf_op jit(solution)/shard_map/reduce_scatter | solution.py:112
  457.1 29.0 %all-gather.21.cloned.1.call-done = bf16[1536,1152]{1,0:T(8,128)(2,1)} async-done(((bf16[192,1152]{1,0:T(8,128)(2,1)}), bf16[1536,1152]{1,0:T(8,128)(2,1)}) %all-gather.21.cloned.1.call-update) | async-done | bytes 3538960 | tf_op jit(solution)/shard_map/all_gather | solution.py:117
  486.1 65.8 %all-gather.19.cloned.1.call-done = bf16[1024,1536]{1,0:T(8,128)(2,1)} async-done(((bf16[256,1536]{1,0:T(8,128)(2,1)}), bf16[1024,1536]{1,0:T(8,128)(2,1)}) %all-gather.19.cloned.1.call-update) | async-done | bytes 3145744 | tf_op jit(solution)/shard_map/all_gather | solution.py:123
  551.9 9.3 fusion.131
  561.2 25.1 %all-gather.23.cloned.1.call-done = bf16[1536,1152]{1,0:T(8,128)(2,1)} async-done(((bf16[192,1152]{1,0:T(8,128)(2,1)}), bf16[1536,1152]{1,0:T(8,128)(2,1)}) %all-gather.23.cloned.1.call-update) | async-done | bytes 3538960 | tf_op jit(solution)/shard_map/all_gather | solution.py:118
  586.3 9.4 fusion.132
  595.7 55.9 %all-gather.27.cloned.1.call-done = bf16[1024,1536]{1,0:T(8,128)(2,1)} async-done(((bf16[256,1536]{1,0:T(8,128)(2,1)}), bf16[1024,1536]{1,0:T(8,128)(2,1)}) %all-gather.27.cloned.1.call-update) | async-done | bytes 3145744 | tf_op jit(solution)/shard_map/all_gather | solution.py:141
  651.5 34.2 %all-gather.25.cloned.1.call-done = bf16[1536,1152]{1,0:T(8,128)(2,1)} async-done(((bf16[192,1152]{1,0:T(8,128)(2,1)}), bf16[1536,1152]{1,0:T(8,128)(2,1)}) %all-gather.25.cloned.1.call-update) | async-done | bytes 3538960 | tf_op jit(solution)/shard_map/all_gather | solution.py:119
  685.8 13.3 multiply_convert_fusion
  703.4 6.3 convolution_add_fusion.1
  709.8 9.6 fusion.133
  719.4 101.4 %reduce-scatter.18.cloned.1.call-done = f32[256,1536]{1,0:T(8,128)} async-done(((f32[1024,1536]{1,0:T(8,128)}), f32[256,1536]{1,0:T(8,128)}) %reduce-scatter.18.cloned.1.call-update) | async-done | bytes 1572880 | tf_op jit(solution)/shard_map/reduce_scatter | solution.py:152
  820.8 113.5 %reduce-scatter.16.cloned.1.call-done = f32[256,1536]{1,0:T(8,128)} async-done(((f32[1024,1536]{1,0:T(8,128)}), f32[256,1536]{1,0:T(8,128)}) %reduce-scatter.16.cloned.1.call-update) | async-done | bytes 1572880 | tf_op jit(solution)/shard_map/reduce_scatter | solution.py:127
  944.3 6.4 slice.639
  963.3 8.9 slice.640
  972.2 8.9 slice.645
  981.0 9.2 slice.638
  1005.1 8.9 fusion.25
  1014.1 16.6 reverse.6
  1152.6 6.3 slice.713
  1195.5 8.6 pad.172
  1207.9 8.7 pad.171
  1220.6 16.7 rev.8
  1247.1 6.8 convert_reduce_fusion.1
  1269.1 8.6 multiply_reduce_fusion.1
  1298.2 9.9 fusion.137
  1308.1 9.9 fusion.138
  1318.2 9.4 convolution_bitcast_fusion
  1327.6 8.1 copy.95
  1360.8 40.3 %all-reduce.47.cloned.1.call-done = f32[8,2048]{1,0:T(8,128)} async-done(((f32[8,2048]{1,0:T(8,128)}), f32[8,2048]{1,0:T(8,128)}) %all-reduce.47.cloned.1.call-update) | async-done | bytes 65552 | tf_op jit(solution)/shard_map/psum | solution.py:230
  1405.6 109.3 %reduce-scatter.20.cloned.1.call-done = f32[256,1536]{1,0:T(8,128)} async-done(((f32[1024,1536]{1,0:T(8,128)}), f32[256,1536]{1,0:T(8,128)}) %reduce-scatter.20.cloned.1.call-update) | async-done | bytes 1572880 | tf_op jit(solution)/shard_map/reduce_scatter | solution.py:212
  1516.7 42.1 %all-reduce.44 = (f32[2,1536]{1,0:T(2,128)S(1)}, f32[4]{0:T(128)S(1)}) all-reduce(f32[2,1536]{1,0:T(2,128)S(1)} %pad_maximum_fusion.15, f32[4]{0:T(128)S(1)} %pad_maximum_fusion.20), channel_id=1, replica_groups=mesh['dp'=8,'tensor'=4] {'dp','tensor'}, use_global_device_ids=true, to_apply=%region_10.11 | all-reduce | flops 3076 | bytes 24608 | tf_op jit(solution)/shard_map/psum | solution.py:230
  1563.8 21.6 %reduce-scatter.30.cloned.1.call-done = f32[192,1152]{1,0:T(8,128)} async-done(((f32[1536,1152]{1,0:T(8,128)}), f32[192,1152]{1,0:T(8,128)}) %reduce-scatter.30.cloned.1.call-update) | async-done | bytes 884752 | tf_op jit(solution)/shard_map/reduce_scatter | solution.py:241
  1585.4 69.9 %reduce-scatter.32.cloned.1.call-done = f32[192,1152]{1,0:T(8,128)} async-done(((f32[1536,1152]{1,0:T(8,128)}), f32[192,1152]{1,0:T(8,128)}) %reduce-scatter.32.cloned.1.call-update) | async-done | bytes 884752 | tf_op jit(solution)/shard_map/reduce_scatter | solution.py:242
  1655.2 69.5 %reduce-scatter.34.cloned.1.call-done = f32[192,1152]{1,0:T(8,128)} async-done(((f32[1536,1152]{1,0:T(8,128)}), f32[192,1152]{1,0:T(8,128)}) %reduce-scatter.34.cloned.1.call-update) | async-done | bytes 884752
  1724.7 38.1 %reduce-scatter.26.cloned.1.call-done = f32[2,4,16,128]{3,2,1,0:T(8,128)} async-done(((f32[2,4,128,128]{3,2,1,0:T(8,128)}), f32[2,4,16,128]{3,2,1,0:T(8,128)}) %reduce-scatter.26.cloned.1.call-update) | async-done | bytes 65552 | tf_op jit(solution)/shard_map/reduce_scatter | solution.py:240
  1762.9 50.1 %reduce-scatter.22.cloned.1.call-done = f32[192,512]{1,0:T(8,128)} async-done(((f32[1536,512]{1,0:T(8,128)}), f32[192,512]{1,0:T(8,128)}) %reduce-scatter.22.cloned.1.call-update) | async-done | bytes 393232 | tf_op jit(solution)/shard_map/reduce_scatter | solution.py:237
  1812.9 50.6 %reduce-scatter.28.cloned.1.call-done = f32[192,512]{1,0:T(8,128)} async-done(((f32[1536,512]{1,0:T(8,128)}), f32[192,512]{1,0:T(8,128)}) %reduce-scatter.28.cloned.1.call-update) | async-done | bytes 393232 | tf_op jit(solution)/shard_map/reduce_scatter | solution.py:239
  1863.5 50.2 %reduce-scatter.24.cloned.1.call-done = f32[192,512]{1,0:T(8,128)} async-done(((f32[1536,512]{1,0:T(8,128)}), f32[192,512]{1,0:T(8,128)}) %reduce-scatter.24.cloned.1.call-update) | async-done | bytes 393232 | tf_op jit(solution)/shard_map/reduce_scatter | solution.py:238
  (523 shorter events, 498.1 us)
Async XLA Ops:
  7.2 30.0 %all-gather.13.cloned.1.call-start = ((), (), s32[]{:S(2)}) async-start(), calls=%async_computation.12 | async-start | bytes 1769472 | tf_op jit(solution)/shard_map/all_gather | solution.py:63
  7.9 94.9 %all-gather.11.cloned.1.call-start = ((), (), s32[]{:S(2)}) async-start(), calls=%async_computation.11 | async-start | bytes 3932160 | tf_op jit(solution)/shard_map/all_gather | solution.py:74
  11.7 315.2 %all-gather.15.cloned.1.call-start = ((), (), s32[]{:S(2)}) async-start(), calls=%async_computation.13 | async-start | bytes 1769472 | tf_op jit(solution)/shard_map/all_gather | solution.py:64
  12.4 322.0 %all-gather.17.cloned.1.call-start = ((), (), s32[]{:S(2)}) async-start(), calls=%async_computation.14 | async-start | bytes 1769472 | tf_op jit(solution)/shard_map/all_gather | solution.py:65
  13.0 437.0 %reduce-scatter.14.cloned.1.call-start = ((), (), s32[]{:S(2)}) async-start(), calls=%async_computation.15 | async-start | bytes 7864320 | tf_op jit(solution)/shard_map/reduce_scatter | solution.py:112
  13.6 93.4 %copy-start.50 = (f32[1,512]{1,0:T(1,128)}, f32[1,512]{1,0:T(1,128)S(1)}, u32[]{:S(2)}) copy-start(f32[1,512]{1,0:T(1,128)S(1)} %get-tuple-element.125) | copy-start | bytes 6148
  13.6 93.4 %copy-start.52 = (f32[1,512]{1,0:T(1,128)}, f32[1,512]{1,0:T(1,128)S(1)}, u32[]{:S(2)}) copy-start(f32[1,512]{1,0:T(1,128)S(1)} %get-tuple-element.126) | copy-start | bytes 6148
  13.6 93.4 %copy-start.54 = (f32[1,512]{1,0:T(1,128)}, f32[1,512]{1,0:T(1,128)S(1)}, u32[]{:S(2)}) copy-start(f32[1,512]{1,0:T(1,128)S(1)} %get-tuple-element.127) | copy-start | bytes 6148
  13.6 93.4 %copy-start.56 = (f32[1,512]{1,0:T(1,128)}, f32[1,512]{1,0:T(1,128)S(1)}, u32[]{:S(2)}) copy-start(f32[1,512]{1,0:T(1,128)S(1)} %get-tuple-element.128) | copy-start | bytes 6148
  23.8 88.9 %copy-start.23 = (bf16[1,4,128,128]{2,3,1,0:T(8,128)(2,1)}, bf16[1,4,128,128]{2,3,1,0:T(8,128)(2,1)S(1)}, u32[]{:S(2)}) copy-start(bf16[1,4,128,128]{2,3,1,0:T(8,128)(2,1)S(1)} %copy.98) | copy-start | bytes 393220
  23.9 93.5 %copy-start.34 = (f32[1,512]{1,0:T(1,128)}, f32[1,512]{1,0:T(1,128)S(1)}, u32[]{:S(2)}) copy-start(f32[1,512]{1,0:T(1,128)S(1)} %get-tuple-element.133) | copy-start | bytes 6148
  23.9 93.5 %copy-start.39 = (f32[1,512]{1,0:T(1,128)}, f32[1,512]{1,0:T(1,128)S(1)}, u32[]{:S(2)}) copy-start(f32[1,512]{1,0:T(1,128)S(1)} %get-tuple-element.134) | copy-start | bytes 6148
  24.5 92.9 %copy-start.41 = (f32[512]{0:T(512)}, f32[512]{0:T(512)S(1)}, u32[]{:S(2)}) copy-start(f32[512]{0:T(512)S(1)} %get-tuple-element.139) | copy-start | bytes 6148
  24.5 83.9 %copy-start.87 = (f32[512]{0:T(512)S(1)}, f32[512]{0:T(512)}, u32[]{:S(2)}) copy-start(f32[512]{0:T(512)} %param.20) | copy-start | bytes 6148
  340.7 113.2 %copy-start.28 = (f32[1536]{0:T(1024)S(1)}, f32[1536]{0:T(1024)}, u32[]{:S(2)}) copy-start(f32[1536]{0:T(1024)} %param.25) | copy-start | bytes 18436
  340.7 145.4 %all-gather.21.cloned.1.call-start = ((), (), s32[]{:S(2)}) async-start(), calls=%async_computation.17 | async-start | bytes 3981312 | tf_op jit(solution)/shard_map/all_gather | solution.py:117
  341.3 210.6 %all-gather.19.cloned.1.call-start = ((), (), s32[]{:S(2)}) async-start(), calls=%async_computation.16 | async-start | bytes 3932160 | tf_op jit(solution)/shard_map/all_gather | solution.py:123
  452.7 486.7 %copy-start.48 = (f32[256]{0:T(256)}, f32[256]{0:T(256)S(1)}, u32[]{:S(2)}) copy-start(f32[256]{0:T(256)S(1)} %add_rsqrt_fusion) | copy-start | bytes 3076
  455.0 131.3 %all-gather.23.cloned.1.call-start = ((), (), s32[]{:S(2)}) async-start(), calls=%async_computation.18 | async-start | bytes 3981312 | tf_op jit(solution)/shard_map/all_gather | solution.py:118
  455.7 195.8 %all-gather.27.cloned.1.call-start = ((), (), s32[]{:S(2)}) async-start(), calls=%async_computation.21 | async-start | bytes 3932160 | tf_op jit(solution)/shard_map/all_gather | solution.py:141
  456.5 229.3 %all-gather.25.cloned.1.call-start = ((), (), s32[]{:S(2)}) async-start(), calls=%async_computation.19 | async-start | bytes 3981312 | tf_op jit(solution)/shard_map/all_gather | solution.py:119
  457.0 363.7 %reduce-scatter.18.cloned.1.call-start = ((), (), s32[]{:S(2)}) async-start(), calls=%async_computation.22 | async-start | bytes 7864320 | tf_op jit(solution)/shard_map/reduce_scatter | solution.py:152
  709.7 224.5 %reduce-scatter.16.cloned.1.call-start = ((), (), s32[]{:S(2)}) async-start(), calls=%async_computation.20 | async-start | bytes 7864320 | tf_op jit(solution)/shard_map/reduce_scatter | solution.py:127
  719.4 285.7 %all-gather.29.cloned.1.call-start = ((), (), s32[]{:S(2)}) async-start(), calls=%async_computation.23 | async-start | bytes 3932160 | tf_op jit(solution)/shard_map/all_gather | solution.py:161
  940.9 460.2 %all-reduce.47.cloned.1.call-start = ((), (), s32[]{:S(2)}) async-start(), calls=%async_computation.27 | async-start | bytes 131072 | tf_op jit(solution)/shard_map/psum | solution.py:230
  1143.8 16.4 copy-start.61
  1143.8 16.4 copy-start.84
  1143.8 16.4 copy-start.85
  1143.8 16.5 copy-start.46
  1143.8 16.5 copy-start.80
  1143.9 16.6 copy-start.37
  1143.9 16.6 copy-start.38
  1143.9 16.6 copy-start.78
  1284.8 230.1 %reduce-scatter.20.cloned.1.call-start = ((), (), s32[]{:S(2)}) async-start(), calls=%async_computation.24 | async-start | bytes 7864320 | tf_op jit(solution)/shard_map/reduce_scatter | solution.py:212
  1298.1 287.3 %reduce-scatter.30.cloned.1.call-start = ((), (), s32[]{:S(2)}) async-start(), calls=%async_computation.30 | async-start | bytes 7962624 | tf_op jit(solution)/shard_map/reduce_scatter | solution.py:241
  1308.0 347.2 %reduce-scatter.32.cloned.1.call-start = ((), (), s32[]{:S(2)}) async-start(), calls=%async_computation.31 | async-start | bytes 7962624 | tf_op jit(solution)/shard_map/reduce_scatter | solution.py:242
  1318.0 406.7 %reduce-scatter.34.cloned.1.call-start = ((), (), s32[]{:S(2)}) async-start(), calls=%async_computation.32 | async-start | bytes 7962624
  1335.7 427.1 %reduce-scatter.26.cloned.1.call-start = ((), (), s32[]{:S(2)}) async-start(), calls=%async_computation.28 | async-start | bytes 589824 | tf_op jit(solution)/shard_map/reduce_scatter | solution.py:240
  1338.7 474.3 %reduce-scatter.22.cloned.1.call-start = ((), (), s32[]{:S(2)}) async-start(), calls=%async_computation.25 | async-start | bytes 3538944 | tf_op jit(solution)/shard_map/reduce_scatter | solution.py:237
  1344.1 519.4 %reduce-scatter.28.cloned.1.call-start = ((), (), s32[]{:S(2)}) async-start(), calls=%async_computation.29 | async-start | bytes 3538944 | tf_op jit(solution)/shard_map/reduce_scatter | solution.py:239
  1350.7 563.1 %reduce-scatter.24.cloned.1.call-start = ((), (), s32[]{:S(2)}) async-start(), calls=%async_computation.26 | async-start | bytes 3538944 | tf_op jit(solution)/shard_map/reduce_scatter | solution.py:238
  1357.2 157.6 %copy-start.6 = (bf16[256,1536]{1,0:T(8,128)(2,1)S(1)}, bf16[256,1536]{1,0:T(8,128)(2,1)}, u32[]{:S(2)}) copy-start(bf16[256,1536]{1,0:T(8,128)(2,1)} %param.15) | copy-start | bytes 2359300
  1357.2 157.6 %copy-start.33 = (f32[1536]{0:T(1024)S(1)}, f32[1536]{0:T(1024)}, u32[]{:S(2)}) copy-start(f32[1536]{0:T(1024)} %param.16) | copy-start | bytes 18436
  1357.2 157.6 %copy-start.63 = (f32[256]{0:T(256)S(1)}, f32[256]{0:T(256)}, u32[]{:S(2)}) copy-start(f32[256]{0:T(256)} %copy-done.62) | copy-start | bytes 3076
  1357.3 202.7 %copy-start.3 = (f32[256,1536]{1,0:T(8,128)S(1)}, f32[256,1536]{1,0:T(8,128)}, u32[]{:S(2)}) copy-start(f32[256,1536]{1,0:T(8,128)} %copy-done.1) | copy-start | bytes 4718596
  1357.3 202.7 %copy-start.19 = (bf16[256,1536]{1,0:T(8,128)(2,1)S(1)}, bf16[256,1536]{1,0:T(8,128)(2,1)}, u32[]{:S(2)}) copy-start(bf16[256,1536]{1,0:T(8,128)(2,1)} %param.29) | copy-start | bytes 2359300
  1357.3 202.6 %copy-start.49 = (f32[256]{0:T(256)S(1)}, f32[256]{0:T(256)}, u32[]{:S(2)}) copy-start(f32[256]{0:T(256)} %copy-done.48) | copy-start | bytes 3076
  1357.3 202.6 %copy-start.65 = (f32[256]{0:T(256)S(1)}, f32[256]{0:T(256)}, u32[]{:S(2)}) copy-start(f32[256]{0:T(256)} %copy-done.64) | copy-start | bytes 3076
  (67 other events, 458.2 us)
Sparse Core Ops, SparseCore 0:
  9.9 27.1 all-gather.12
  39.3 63.5 all-gather.10
  104.8 24.2 all-gather.14
  130.8 25.6 all-gather.16
  340.8 109.1 reduce-scatter.13
  451.7 34.3 all-gather.20
  488.2 63.6 all-gather.18
  553.8 32.4 all-gather.22
  587.9 63.6 all-gather.26
  653.3 32.4 all-gather.24
  709.9 110.8 reduce-scatter.17
  822.9 111.2 reduce-scatter.15
  941.1 64.0 all-gather.28
  1284.9 116.1 all-reduce.46
  1403.3 111.5 reduce-scatter.19
  1518.8 66.5 reduce-scatter.29
  1589.7 65.4 reduce-scatter.31
  1659.2 65.4 reduce-scatter.33
  1728.7 34.1 reduce-scatter.25
  1766.7 46.2 reduce-scatter.21
  1817.3 46.1 reduce-scatter.27
  1867.5 46.2 reduce-scatter.23
where the time goes:
time: 1950 us; the launch traced here: 1920 us
  waiting for transfers between devices  1120 us (57%)
  local copies, waits for them, and re-layouts  442 us (23%)
  other arithmetic  150 us (8%)
  matrix products  138 us (7%)
  blocking collectives  51.8 us (3%)
    slice x63, local copies, waits for them, and re-layouts, local(): lax.associative_scan(combine, (next_decay, d_states.reshape(seq_count, SE...  156 us
    slice x60, local copies, waits for them, and re-layouts, local(): lax.associative_scan(combine, (seq_decay, inflow.reshape(seq_count, SEQ_L...  127 us
    reduce_scatter x1, waiting for transfers between devices, local(): lax.psum_scatter(back_product(hidden, mlp_d), 'tensor', scatter_dimension...  113 us
    reduce_scatter x1, waiting for transfers between devices, local(): lax.psum_scatter(back_product(d_x_low, rec_x) + back_product(d_y_low, rec...  109 us
    reduce_scatter x1, waiting for transfers between devices, local(): lax.psum_scatter(back_product(mixed_out, rec_o), 'tensor', scatter_dimens...  109 us
    reduce_scatter x1, waiting for transfers between devices, local(): lax.psum_scatter(back_product(d_gate_low, mlp_g) + back_product(d_up_low,...  101 us
    unnamed x23, waiting for transfers between devices  74 us
    reduce_scatter x1, waiting for transfers between devices, local(): lax.psum_scatter(mlp_summed[1], 'dp', scatter_dimension=0, tiled=True)  69.9 us
  transfers between devices with their start and end apart: 22, of which 20 were waited for; matrix products, arithmetic and copies ran while one was open for 21% of the time, Pallas kernels for 0%

commit v1 on v0

--- a/solution.py
+++ b/solution.py
@@ -1,6 +1,8 @@
 import jax
 import jax.numpy as jnp
 from jax import lax
+from jax.experimental import pallas as pl
+from jax.experimental.pallas import tpu as pltpu
 from jax.sharding import PartitionSpec as P
 
 CONV = 4
@@ -264,9 +266,1474 @@
     )
 
 
+MESH = pl.DeviceIdType.MESH
+bf16 = jnp.bfloat16
+f32 = jnp.float32
+VMEM_BYTES = 67043328
+
+
+def mm(a, b):
+    return jnp.dot(a, b, preferred_element_type=f32)
+
+
+def mm_nt(a, b):
+    return lax.dot_general(a, b, (((1,), (1,)), ((), ())), preferred_element_type=f32)
+
+
+def mm_tn(a, b):
+    return lax.dot_general(a, b, (((0,), (0,)), ((), ())), preferred_element_type=f32)
+
+
+def gelu_value(x):
+    return 0.5 * x * (1.0 + jnp.tanh(0.7978845608028654 * x * (1.0 + 0.044715 * (x * x))))
+
+
+def gelu_pair(x):
+    x2 = x * x
+    th = jnp.tanh(0.7978845608028654 * x * (1.0 + 0.044715 * x2))
+    cdf = 0.5 * (1.0 + th)
+    slope = 0.5 * x * (1.0 - th * th) * (0.7978845608028654 * (1.0 + 0.134145 * x2))
+    return x * cdf, cdf + slope
+
+
+def neg_expm1(x):
+    series = x * (
+        1.0
+        + x * (0.5 + x * (1 / 6 + x * (1 / 24 + x * (1 / 120 + x * (1 / 720 + x * (1 / 5040))))))
+    )
+    return -jnp.where(x > -0.35, series, jnp.exp(x) - 1.0)
+
+
+class Place:
+    def __init__(self):
+        self.d = lax.axis_index("dp")
+        self.z = lax.axis_index("tensor")
+        self.t = lax.div(self.d, 2)
+        self.c = lax.rem(self.d, 2)
+        self.tx = self.t + 1 - 2 * lax.rem(self.t, 2)
+        self.ty = self.t + 2 - 4 * lax.div(self.t, 2)
+        self.td = 3 - self.t
+        self.peers = (self.tx, self.ty, self.td)
+
+    def plane(self, t):
+        return (2 * t + self.c, self.z)
+
+    def line(self, z):
+        return (self.d, z)
+
+    def partner(self):
+        return (2 * self.t + 1 - self.c, self.z)
+
+    def around(self, k):
+        return lax.rem(self.z + k, 4)
+
+    def enter(self):
+        barrier = pltpu.get_barrier_semaphore()
+        targets = [self.plane(t) for t in self.peers] + [self.partner()]
+        targets += [self.line(self.around(k)) for k in (1, 2, 3)]
+        for target in targets:
+            pl.semaphore_signal(barrier, inc=1, device_id=target, device_id_type=MESH)
+        pl.semaphore_wait(barrier, len(targets))
+
+
+class Wires:
+    def __init__(self, place, send, recv, local):
+        self.place, self.send, self.recv, self.local = place, send, recv, local
+        self.used, self.used_local = 0, 0
+
+    def slot(self):
+        self.used += 1
+        assert self.used <= self.send.shape[0]
+        return self.used - 1
+
+    def copy(self, src, dst, slot, device):
+        return pltpu.make_async_remote_copy(
+            src_ref=src,
+            dst_ref=dst,
+            send_sem=self.send.at[slot],
+            recv_sem=self.recv.at[slot],
+            device_id=device,
+            device_id_type=MESH,
+        )
+
+    def landed(self, ref, slot):
+        self.copy(ref, ref, slot, self.place.partner()).wait_recv()
+
+    def sent(self, ref, slot):
+        self.copy(ref, ref, slot, self.place.partner()).wait_send()
+
+    def held_here(self, src, dst):
+        self.used_local += 1
+        assert self.used_local <= self.local.shape[0]
+        return pltpu.make_async_copy(src, dst, self.local.at[self.used_local - 1])
+
+    def here(self, src, dst):
+        made = self.held_here(src, dst)
+        made.start()
+        return made
+
+
+class Spread:
+    def __init__(self, w, parts, homes):
+        self.w, self.parts, self.homes = w, parts, homes
+        self.slots = [[w.slot() for _ in range(3)] for _ in parts]
+
+    def start(self):
+        p = self.w.place
+        self.local = []
+        for part, home, slots in zip(self.parts, self.homes, self.slots):
+            for peer, slot in zip(p.peers, slots):
+                self.w.copy(part(peer), home(p.t), slot, p.plane(peer)).start()
+            self.local.append(self.w.here(part(p.t), home(p.t)))
+
+    def wait(self):
+        p = self.w.place
+        for made in self.local:
+            made.wait()
+        for home, slots in zip(self.homes, self.slots):
+            for peer, slot in zip(p.peers, slots):
+                self.w.landed(home(peer), slot)
+
+    def drain(self):
+        p = self.w.place
+        for part, slots in zip(self.parts, self.slots):
+            for peer, slot in zip(p.peers, slots):
+                self.w.sent(part(peer), slot)
+
+
+class OneSpread:
+    def __init__(self, w, part, home):
+        self.w, self.part, self.home = w, part, home
+        self.slots = [w.slot() for _ in range(3)]
+        self.kept = w.held_here(part, home(w.place.t))
+
+    def start(self):
+        p = self.w.place
+
+        @pl.when(p.t == p.z)
+        def _():
+            self.kept.start()
+
+        for peer, slot in zip(p.peers, self.slots):
+
+            @pl.when(peer == p.z)
+            def _():
+                self.w.copy(self.part, self.home(p.t), slot, p.plane(peer)).start()
+
+    def wait(self):
+        p = self.w.place
+
+        @pl.when(p.t == p.z)
+        def _():
+            self.kept.wait()
+            for peer, slot in zip(p.peers, self.slots):
+                self.w.landed(self.home(peer), slot)
+
+    def drain(self):
+        p = self.w.place
+        for peer, slot in zip(p.peers, self.slots):
+
+            @pl.when(peer == p.z)
+            def _():
+                self.w.sent(self.part, slot)
+
+
+class LineGather:
+    def __init__(self, w, regions):
+        self.w, self.regions = w, regions
+        self.slots = [
+            {key: w.slot() for key in ["o", "r1", "r2", "r3", "l1", "l2", "l3"]
+             + ["or1", "or2", "or3", "ol1", "ol2", "ol3"]}
+            for _ in regions
+        ]
+
+    def _each(self, b, act, *conditions):
+        p = self.w.place
+        for (view, odd), slots in zip(self.regions, self.slots):
+            terms = list(conditions) + ([b == p.t] if odd else [])
+            if not terms:
+                act(view, slots)
+                continue
+            ok = terms[0]
+            for term in terms[1:]:
+                ok = jnp.logical_and(ok, term)
+
+            @pl.when(ok)
+            def _():
+                act(view, slots)
+
+    def _start(self, view, b, slot, device):
+        p = self.w.place
+        self.w.copy(view(b, p.c), view(b, p.c), slot, device).start()
+
+    def first(self):
+        p = self.w.place
+        z = p.z
+        self._each(z, lambda v, s: self._start(v, z, s["r1"], p.line(z + 1)), z < 3)
+        self._each(z, lambda v, s: self._start(v, z, s["l1"], p.line(z - 1)), z > 0)
+        self._each(z, lambda v, s: self._start(v, z, s["o"], p.partner()))
+
+    def step(self, k):
+        p = self.w.place
+        z = p.z
+        for sign, left in ((1, "r"), (-1, "l")):
+            b = z - sign * (k - 1)
+            exists = b >= 0 if sign > 0 else b <= 3
+
+            def take(v, s):
+                self.w.landed(v(b, p.c), s[f"{left}{k - 1}"])
+                self._start(v, b, s[f"o{left}{k - 1}"], p.partner())
+
+            self._each(b, take, exists)
+            if k < 4:
+                more = z < 3 if sign > 0 else z > 0
+                self._each(
+                    b, lambda v, s: self._start(v, b, s[f"{left}{k}"], p.line(z + sign)), exists, more
+                )
+
+    def finish(self):
+        p = self.w.place
+        z = p.z
+        other = 1 - p.c
+        self._each(z, lambda v, s: self.w.landed(v(z, other), s["o"]))
+        for k in (1, 2, 3):
+            for sign, left in ((1, "r"), (-1, "l")):
+                b = z - sign * k
+                exists = b >= 0 if sign > 0 else b <= 3
+                self._each(b, lambda v, s: self.w.landed(v(b, other), s[f"o{left}{k}"]), exists)
+
+    def drain(self):
+        p = self.w.place
+        z = p.z
+        self._each(z, lambda v, s: self.w.sent(v(z, p.c), s["o"]))
+        for k in (1, 2, 3):
+            for sign, left in ((1, "r"), (-1, "l")):
+                b = z - sign * k
+                exists = b >= 0 if sign > 0 else b <= 3
+                self._each(b, lambda v, s: self.w.sent(v(b, p.c), s[f"o{left}{k}"]), exists)
+                b2 = z - sign * (k - 1)
+                exists2 = b2 >= 0 if sign > 0 else b2 <= 3
+                more = z < 3 if sign > 0 else z > 0
+                self._each(b2, lambda v, s: self.w.sent(v(b2, p.c), s[f"{left}{k}"]), exists2, more)
+
+
+class PlaneGather:
+    def __init__(self, w, buf):
+        self.w, self.buf = w, buf
+        self.half = buf.shape[1] // 2
+        self.s = {key: w.slot() for key in ("x", "y", "fx", "fy")}
+
+    def _low(self, t):
+        return self.buf.at[t, pl.ds(0, self.half)]
+
+    def _high(self, t):
+        return self.buf.at[t, pl.ds(self.half, self.half)]
+
+    def start(self, own=None):
+        p, w = self.w.place, self.w
+        self.own = self.buf.at[p.t] if own is None else own
+        w.copy(self.own, self.buf.at[p.t], self.s["x"], p.plane(p.tx)).start()
+        w.copy(self.own, self.buf.at[p.t], self.s["y"], p.plane(p.ty)).start()
+
+    def forward(self):
+        p, w = self.w.place, self.w
+        w.landed(self.buf.at[p.tx], self.s["x"])
+        w.copy(self._high(p.tx), self._high(p.tx), self.s["fy"], p.plane(p.ty)).start()
+        w.landed(self.buf.at[p.ty], self.s["y"])
+        w.copy(self._low(p.ty), self._low(p.ty), self.s["fx"], p.plane(p.tx)).start()
+
+    def finish(self):
+        p, w = self.w.place, self.w
+        w.landed(self._low(p.td), self.s["fx"])
+        w.landed(self._high(p.td), self.s["fy"])
+
+    def drain(self):
+        p, w = self.w.place, self.w
+        w.sent(self.own, self.s["x"])
+        w.sent(self.own, self.s["y"])
+        w.sent(self._high(p.tx), self.s["fy"])
+        w.sent(self._low(p.ty), self.s["fx"])
+
+
+class PlaneSum:
+    def __init__(self, w, part, far, near):
+        self.w, self.part, self.far, self.near = w, part, far, near
+        self.half = part.shape[1] // 2
+        self.s = {key: w.slot() for key in ("dx", "dy", "x", "y")}
+
+    def diagonal(self):
+        p, w, h = self.w.place, self.w, self.half
+        self.a = self.part.at[p.td, pl.ds(0, h)]
+        self.b = self.part.at[p.td, pl.ds(h, h)]
+        w.copy(self.a, self.far.at[0], self.s["dx"], p.plane(p.tx)).start()
+        w.copy(self.b, self.far.at[1], self.s["dy"], p.plane(p.ty)).start()
+
+    def _add(self, t, which):
+        h = self.half
+
+        @pl.loop(0, h // 32)
+        def _(i):
+            rows = pl.ds(pl.multiple_of(i * 32, 32), 32)
+            mine = pl.ds(pl.multiple_of(which * h + i * 32, 32), 32)
+            total = self.part[t, mine, :].astype(f32) + self.far[which, rows, :].astype(f32)
+            self.part[t, mine, :] = total.astype(bf16)
+
+    def to_y(self):
+        p, w = self.w.place, self.w
+        w.landed(self.far.at[0], self.s["dx"])
+        self._add(p.ty, 0)
+        w.copy(self.part.at[p.ty], self.near.at[1], self.s["y"], p.plane(p.ty)).start()
+
+    def to_x(self):
+        p, w = self.w.place, self.w
+        w.landed(self.far.at[1], self.s["dy"])
+        self._add(p.tx, 1)
+        w.copy(self.part.at[p.tx], self.near.at[0], self.s["x"], p.plane(p.tx)).start()
+
+    def finish(self):
+        self.w.landed(self.near.at[0], self.s["x"])
+        self.w.landed(self.near.at[1], self.s["y"])
+
+    def drain(self):
+        p, w = self.w.place, self.w
+        w.sent(self.a, self.s["dx"])
+        w.sent(self.b, self.s["dy"])
+        w.sent(self.part.at[p.ty], self.s["y"])
+        w.sent(self.part.at[p.tx], self.s["x"])
+
+
+def add_into(dst, src):
+    shape = dst.shape
+    if len(shape) == 2:
+        dst[...] = (dst[...].astype(f32) + src[...].astype(f32)).astype(bf16)
+        return
+    for i in range(shape[0]):
+        add_into(dst.at[i], src.at[i])
+
+
+class CoreSum:
+    def __init__(self, w, half, landing):
+        self.w, self.half, self.landing = w, half, landing
+        self.slot = w.slot()
+
+    def start(self):
+        p = self.w.place
+        self.w.copy(self.half(1 - p.c), self.landing, self.slot, p.partner()).start()
+
+    def finish(self):
+        self.w.landed(self.landing, self.slot)
+        add_into(self.half(self.w.place.c), self.landing)
+
+    def drain(self):
+        self.w.sent(self.half(1 - self.w.place.c), self.slot)
+
+
+class LineSum:
+    def __init__(self, w, regions):
+        self.w, self.regions = w, regions
+        self.slots = [[w.slot() for _ in range(6)] for _ in regions]
+
+    def _each(self, j, act, *conditions):
+        p = self.w.place
+        for (piece, landing, odd), slots in zip(self.regions, self.slots):
+            terms = list(conditions) + ([j == p.t] if odd else [])
+            ok = terms[0]
+            for term in terms[1:]:
+                ok = jnp.logical_and(ok, term)
+
+            @pl.when(ok)
+            def _():
+                act(piece, landing, slots)
+
+    def _send(self, k, act):
+        z = self.w.place.z
+        for side, sign in ((0, 1), (1, -1)):
+            j = z + sign * (4 - k)
+            valid = jnp.logical_and(j <= 3, z < 3) if sign > 0 else jnp.logical_and(j >= 0, z > 0)
+            self._each(j, lambda piece, landing, s: act(piece, landing, s[side * 3 + k - 1], side, k, j, sign), valid)
+
+    def _out(self, piece, landing, slot, side, k, j, sign):
+        p = self.w.place
+        self.w.copy(piece(j), landing(side, k), slot, p.line(p.z + sign)).start()
+
+    def first(self):
+        self._send(1, self._out)
+
+    def _take(self, k):
+        z = self.w.place.z
+        for side, sign in ((0, 1), (1, -1)):
+            j = z - sign + sign * (4 - k)
+            valid = jnp.logical_and(j <= 3, z >= 1) if sign > 0 else jnp.logical_and(j >= 0, z <= 2)
+
+            def act(piece, landing, s):
+                self.w.landed(landing(side, k), s[side * 3 + k - 1])
+                add_into(piece(j), landing(side, k))
+
+            self._each(j, act, valid)
+
+    def step(self, k):
+        self._take(k - 1)
+        if k < 4:
+            self._send(k, self._out)
+
+    def drain(self):
+        for k in (1, 2, 3):
+            self._send(k, lambda piece, landing, slot, side, kk, j, sign: self.w.sent(piece(j), slot))
+
+
+def rows16(i, size=16):
+    return pl.ds(pl.multiple_of(i * 16, 16), size)
+
+
+def recurrence_forward(
+    x_ref, gain_ref, small_ref, wx, wy, wo, gates, wg, wu, wd,
+    x1_ref, stat_ref, sm_out,
+    n1_out, win_out, wout_out, wg_out, a2u, a2d, gg_out,
+    xb_out, zy_out, zx_out, za_out, c_out, a_out, h_out, o_out,
+    win, wout, gg, n1, xb, zy, zx, za, cc, aa, hh, ac, oo, part, far, near, own,
+    tail, sums, hin, sm_ref, send, recv, local,
+):
+    p = Place()
+    w = Wires(p, send, recv, local)
+    t, c, z = p.t, p.c, p.z
+    p.enter()
+
+    def cols(b, width=128):
+        return pl.ds(pl.multiple_of(b * width, width), width)
+
+    spread_in = Spread(
+        w,
+        [lambda q: wx.at[:, cols(q)], lambda q: wy.at[:, cols(q)], lambda q: gates.at[:, q]],
+        [
+            lambda q: win.at[0, q, c, :, cols(z)],
+            lambda q: win.at[1, q, c, :, cols(z)],
+            lambda q: gg.at[:, z, q, c],
+        ],
+    )
+    spread_out = Spread(
+        w, [lambda q: wo.at[:, cols(q)]], [lambda q: wout.at[q, c, :, cols(z)]]
+    )
+    spread_g = Spread(
+        w, [lambda q: wg.at[:, cols(q, 256)]], [lambda q: wg_out.at[q, c, :, cols(z, 256)]]
+    )
+    odd_g = OneSpread(w, wg.at[:, pl.ds(1024, 128)], lambda q: wg_out.at[q, c, :, pl.ds(1024, 128)])
+    spread_ud = Spread(
+        w,
+        [lambda q: wu.at[:, cols(q, 256)], lambda q: wd.at[:, cols(q, 256)]],
+        [lambda q: a2u.at[q, :, pl.ds(0, 256)], lambda q: a2d.at[q, :, pl.ds(0, 256)]],
+    )
+    odd_u = OneSpread(w, wu.at[:, pl.ds(1024, 128)], lambda q: a2u.at[q, :, pl.ds(256, 128)])
+    odd_d = OneSpread(w, wd.at[:, pl.ds(1024, 128)], lambda q: a2d.at[q, :, pl.ds(256, 128)])
+
+    spread_in.start()
+    spread_out.start()
+    small_slots = [w.slot() for _ in range(3)]
+    for k in (1, 2, 3):
+        w.copy(
+            small_ref.at[:, cols(t)], sm_ref.at[:, cols(z)], small_slots[k - 1], p.line(p.around(k))
+        ).start()
+    sm_ref[:, cols(z)] = small_ref[:, cols(t)]
+
+    @pl.loop(0, 16)
+    def _(i):
+        v = x_ref[rows16(i), :].astype(f32)
+        s = lax.rsqrt(jnp.mean(v * v, axis=1, keepdims=True) + epsilon)
+        n1[t, rows16(i), :] = (v * s * gain_ref[...]).astype(bf16)
+
+    gather = PlaneGather(w, n1)
+    gather.start()
+
+    spread_in.wait()
+    line_in = LineGather(
+        w,
+        [
+            (lambda b, q: win.at[:, :, q, :, cols(b)], False),
+            (lambda b, q: gg.at[:, b, :, q], False),
+        ],
+    )
+    line_in.first()
+    spread_out.wait()
+    line_out = LineGather(w, [(lambda b, q: wout.at[:, q, :, cols(b)], False)])
+    line_in.step(2)
+    gather.forward()
+    line_in.step(3)
+    line_out.first()
+    spread_g.start()
+    odd_g.start()
+    line_in.step(4)
+    line_in.finish()
+    kept = [w.here(win, win_out), w.here(gg, gg_out)]
+    gather.finish()
+    kept.append(w.here(n1, n1_out))
+    spread_ud.start()
+    odd_u.start()
+    odd_d.start()
+
+    @pl.loop(0, 4)
+    def _(j):
+        xb[j, pl.ds(8, 256), :] = mm(n1[j], win[0].reshape(1536, 512))
+        zy[j] = mm(n1[j], win[1].reshape(1536, 512))
+
+    kept.append(w.here(zy, zy_out))
+    halo = w.slot()
+
+    @pl.when(z < 3)
+    def _():
+        w.copy(xb.at[:, pl.ds(256, 8)], xb.at[:, pl.ds(0, 8)], halo, p.line(z + 1)).start()
+
+    @pl.when(z == 0)
+    def _():
+        xb[:, 0:8, :] = jnp.zeros((4, 8, 512), f32)
+
+    line_out.step(2)
+    spread_g.wait()
+    odd_g.wait()
+    line_g = LineGather(
+        w,
+        [
+            (lambda b, q: wg_out.at[:, q, :, cols(b, 256)], False),
+            (lambda b, q: wg_out.at[:, q, :, pl.ds(1024, 128)], True),
+        ],
+    )
+    for k in (1, 2, 3):
+        w.landed(sm_ref.at[:, cols(p.around(4 - k))], small_slots[k - 1])
+
+    @pl.when(z > 0)
+    def _():
+        w.landed(xb.at[:, pl.ds(0, 8)], halo)
+
+    @pl.loop(0, 4)
+    def _(j):
+        @pl.loop(0, 16)
+        def _(i):
+            v = xb[j, rows16(i, 24), :]
+            total = sm_ref[4:5, :] + sm_ref[0:1, :] * v[8:24]
+            for k in (1, 2, 3):
+                total = total + sm_ref[k : k + 1, :] * v[8 - k : 24 - k]
+            cc[j, rows16(i), :] = total.astype(bf16)
+
+        for b in range(4):
+            lanes = pl.ds(b * 128, 128)
+            left = cc[j, :, lanes]
+            zx[j, :, lanes] = mm(left, gg[0, b].reshape(128, 128)) + sm_ref[5:6, lanes]
+            za[j, :, lanes] = mm(left, gg[1, b].reshape(128, 128)) + sm_ref[6:7, lanes]
+
+    kept += [w.here(xb, xb_out), w.here(cc, c_out), w.here(zx, zx_out), w.here(za, za_out)]
+    line_out.step(3)
+    line_g.first()
+
+    row = lax.broadcasted_iota(jnp.int32, (8, 512), 0)
+    zero = jnp.zeros((8, 512), f32)
+
+    def advance(i, carry):
+        result = []
+        for s in range(4):
+            state, product = carry[s]
+            pre_x, pre_a = zx[s, rows16(i), :], za[s, rows16(i), :]
+            log_a = -8.0 * jax.nn.sigmoid(pre_a) * sm_ref[7:8, :]
+            decay = jnp.exp(log_a)
+            mult = jnp.sqrt(neg_expm1(2.0 * log_a))
+            index = lax.broadcasted_iota(jnp.int32, (16, 512), 0) + i * 16 + z * 256
+            mult = jnp.where(index == 0, 1.0, mult)
+            inflow = mult * jax.nn.sigmoid(pre_x) * cc[s, rows16(i), :].astype(f32)
+            aa[s, rows16(i), :] = decay
+            for half in (0, 8):
+                dv, uv = decay[half : half + 8], inflow[half : half + 8]
+                for st in (1, 2, 4):
+                    ok = row >= st
+                    uv = uv + jnp.where(ok, dv * pltpu.roll(uv, st, 0), 0.0)
+                    dv = jnp.where(ok, dv * pltpu.roll(dv, st, 0), dv)
+                hv, pv = uv + dv * state, dv * product
+                at = pl.ds(pl.multiple_of(i * 16 + half, 8), 8)
+                hh[s, pl.ds(pl.multiple_of(i * 16 + half + 8, 8), 8), :] = hv
+                ac[s, at, :] = pv
+                state = jnp.broadcast_to(hv[7:8, :], (8, 512))
+                product = jnp.broadcast_to(pv[7:8, :], (8, 512))
+            result.append((state, product))
+        return tuple(result)
+
+    ends = lax.fori_loop(0, 16, advance, tuple((zero, zero + 1.0) for _ in range(4)))
+    for s in range(4):
+        tail[s, 0:8, :] = ends[s][0]
+        tail[s, 8:16, :] = ends[s][1]
+
+    base = [w.slot() for _ in range(3)]
+    for away in (1, 2, 3):
+
+        @pl.when(z + away <= 3)
+        def _():
+            w.copy(tail, sums.at[z], base[away - 1], p.line(z + away)).start()
+
+    next_slot = w.slot()
+
+    @pl.when(z > 0)
+    def _():
+        w.copy(aa.at[:, pl.ds(0, 8)], aa.at[:, pl.ds(256, 8)], next_slot, p.line(z - 1)).start()
+
+    @pl.when(z == 3)
+    def _():
+        aa[:, 256:264, :] = jnp.zeros((4, 8, 512), f32)
+
+    line_out.step(4)
+    line_out.finish()
+    kept.append(w.here(wout, wout_out))
+    hin[...] = jnp.zeros((4, 8, 512), f32)
+    for away in (1, 2, 3):
+
+        @pl.when(z >= away)
+        def _():
+            w.landed(sums.at[z - away], base[away - 1])
+
+    for src in range(3):
+
+        @pl.when(z > src)
+        def _():
+            hin[...] = sums[src, :, 0:8, :] + sums[src, :, 8:16, :] * hin[...]
+
+    line_g.step(2)
+
+    @pl.loop(0, 4)
+    def _(j):
+        enter = hin[j]
+        hh[j, 0:8, :] = enter
+        first = jnp.concatenate([enter, enter], axis=0)
+
+        @pl.loop(0, 16)
+        def _(i):
+            at = pl.ds(pl.multiple_of(i * 16 + 8, 8), 16)
+            hv = hh[j, at, :] + ac[j, rows16(i), :] * first
+            hh[j, at, :] = hv
+            oo[j, rows16(i), :] = (hv * gelu_value(zy[j, rows16(i), :])).astype(bf16)
+
+    kept += [w.here(hh, h_out), w.here(oo, o_out)]
+
+    @pl.when(z < 3)
+    def _():
+        w.landed(aa.at[:, pl.ds(256, 8)], next_slot)
+
+    kept.append(w.here(aa, a_out))
+
+    def project(j):
+        for n in range(2):
+            part[j, :, n * 768 : (n + 1) * 768] = mm_nt(
+                oo[j], wout[2 * n : 2 * n + 2].reshape(768, 512)
+            ).astype(bf16)
+
+    summed = PlaneSum(w, part, far, near)
+    project(p.td)
+    summed.diagonal()
+    project(p.ty)
+    project(p.tx)
+    summed.to_y()
+    summed.to_x()
+    for n in range(2):
+        own[:, n * 768 : (n + 1) * 768] = mm_nt(
+            oo[t], wout[2 * n : 2 * n + 2].reshape(768, 512)
+        )
+    line_g.step(3)
+    summed.finish()
+
+    def last(i, carry):
+        at = rows16(i)
+        branch = own[at, :] + near[0, at, :].astype(f32) + near[1, at, :].astype(f32)
+        stream = x_ref[at, :].astype(f32) + branch
+        x1_ref[at, :] = stream
+        s2, b2 = stream * stream, branch * branch
+        return carry[0] + s2[0:8] + s2[8:16], carry[1] + b2[0:8] + b2[8:16]
+
+    zw = jnp.zeros((8, 1536), f32)
+    s2, b2 = lax.fori_loop(0, 16, last, (zw, zw))
+    stat_ref[...] = zw
+    stat_ref[0:1, :] = jnp.sum(s2, axis=0, keepdims=True)
+    stat_ref[1:2, :] = jnp.sum(b2, axis=0, keepdims=True)
+    sm_out[...] = sm_ref[...]
+
+    line_g.step(4)
+    line_g.finish()
+    spread_ud.wait()
+    odd_u.wait()
+    odd_d.wait()
+    for made in kept:
+        made.wait()
+    spread_in.drain()
+    spread_out.drain()
+    spread_g.drain()
+    odd_g.drain()
+    spread_ud.drain()
+    odd_u.drain()
+    odd_d.drain()
+    for k in (1, 2, 3):
+        w.sent(small_ref.at[:, cols(t)], small_slots[k - 1])
+    gather.drain()
+    line_in.drain()
+    line_out.drain()
+    line_g.drain()
+
+    @pl.when(z < 3)
+    def _():
+        w.sent(xb.at[:, pl.ds(256, 8)], halo)
+
+    for away in (1, 2, 3):
+
+        @pl.when(z + away <= 3)
+        def _():
+            w.sent(tail, base[away - 1])
+
+    @pl.when(z > 0)
+    def _():
+        w.sent(aa.at[:, pl.ds(0, 8)], next_slot)
+
+    summed.drain()
+
+
+def shape(dims, dtype):
+    return jax.ShapeDtypeStruct(dims, dtype)
+
+
+def call(kernel, number, args, spaces, outs, out_spaces, scratch, wires, locals_, name):
+    v = pl.BlockSpec(memory_space=pltpu.VMEM)
+    a = pl.BlockSpec(memory_space=pl.ANY)
+    kinds = {"v": v, "a": a}
+    return pl.pallas_call(
+        kernel,
+        out_shape=outs,
+        in_specs=[kinds[k] for k in spaces],
+        out_specs=[kinds[k] for k in out_spaces],
+        scratch_shapes=list(scratch)
+        + [
+            pltpu.SemaphoreType.DMA((wires,)),
+            pltpu.SemaphoreType.DMA((wires,)),
+            pltpu.SemaphoreType.DMA((locals_,)),
+        ],
+        compiler_params=pltpu.CompilerParams(
+            collective_id=number, has_side_effects=True, vmem_limit_bytes=VMEM_BYTES
+        ),
+        name=name,
+    )(*args)
+
+
+def forward_recurrence(x, g1, small, wx, wy, wo, gates, wg, wu, wd):
+    V = pltpu.VMEM
+    outs = [
+        shape((256, 1536), f32), shape((8, 1536), f32), shape((16, 512), f32),
+        shape((4, 256, 1536), bf16), shape((2, 4, 2, 192, 512), bf16), shape((4, 2, 192, 512), bf16),
+        shape((4, 2, 192, 1152), bf16), shape((4, 192, 384), bf16), shape((4, 192, 384), bf16),
+        shape((2, 4, 4, 2, 16, 128), bf16),
+        shape((4, 264, 512), f32), shape((4, 256, 512), f32), shape((4, 256, 512), f32),
+        shape((4, 256, 512), f32), shape((4, 256, 512), bf16), shape((4, 264, 512), f32),
+        shape((4, 264, 512), f32), shape((4, 256, 512), bf16),
+    ]
+    scratch = [
+        V((2, 4, 2, 192, 512), bf16), V((4, 2, 192, 512), bf16), V((2, 4, 4, 2, 16, 128), bf16),
+        V((4, 256, 1536), bf16), V((4, 264, 512), f32), V((4, 256, 512), f32),
+        V((4, 256, 512), f32), V((4, 256, 512), f32), V((4, 256, 512), bf16),
+        V((4, 264, 512), f32), V((4, 264, 512), f32), V((4, 256, 512), f32),
+        V((4, 256, 512), bf16), V((4, 256, 1536), bf16), V((2, 128, 1536), bf16),
+        V((2, 256, 1536), bf16), V((256, 1536), f32),
+        V((4, 16, 512), f32), V((4, 4, 16, 512), f32), V((4, 8, 512), f32), V((16, 512), f32),
+    ]
+    return call(
+        recurrence_forward, 0, (x, g1, small, wx, wy, wo, gates, wg, wu, wd), "vvvaaaaaaa",
+        outs, "vvv" + "a" * 15, scratch, 128, 32, "recurrence_forward",
+    )
+
+
+class OddScatter:
+    def __init__(self, w, part, home):
+        self.w, self.part, self.home = w, part, home
+        self.slots = [w.slot() for _ in range(3)]
+        self.kept = w.held_here(part(w.place.t), home)
+
+    def start(self):
+        p = self.w.place
+
+        @pl.when(p.t == p.z)
+        def _():
+            self.kept.start()
+            for peer, slot in zip(p.peers, self.slots):
+                self.w.copy(self.part(peer), self.home, slot, p.plane(peer)).start()
+
+    def finish(self):
+        p = self.w.place
+        for peer, slot in zip(p.peers, self.slots):
+
+            @pl.when(peer == p.z)
+            def _():
+                self.w.landed(self.home, slot)
+
+        @pl.when(p.t == p.z)
+        def _():
+            self.kept.wait()
+            for peer, slot in zip(p.peers, self.slots):
+                self.w.sent(self.part(peer), slot)
+
+
+def cols(b, width=128):
+    return pl.ds(pl.multiple_of(b * width, width), width)
+
+
+def norm_rows(v):
+    return lax.rsqrt(jnp.mean(v * v, axis=1, keepdims=True) + epsilon)
+
+
+def feed_forward(
+    x1_ref, gain_ref, cot, wg_in, a2u, a2d,
+    dx1_ref, y_ref, stat_ref, half_out, gd_out,
+    wg, wu, wd, n2, ct, gate, up, hid, dga, dup, part, far, near, far2, near2, own, own2,
+    gdown, cb, landing, landing_odd, send, recv, local,
+):
+    p = Place()
+    w = Wires(p, send, recv, local)
+    t, c, z = p.t, p.c, p.z
+    p.enter()
+    odd = pl.ds(1024, 128)
+
+    first = [
+        w.here(a2u.at[:, :, pl.ds(0, 256)], wu.at[:, c, :, cols(z, 256)]),
+        w.here(a2d.at[:, :, pl.ds(0, 256)], wd.at[:, c, :, cols(z, 256)]),
+    ]
+    first_odd = [
+        w.held_here(a2u.at[:, :, pl.ds(256, 128)], wu.at[:, c, :, odd]),
+        w.held_here(a2d.at[:, :, pl.ds(256, 128)], wd.at[:, c, :, odd]),
+    ]
+
+    @pl.when(t == z)
+    def _():
+        for made in first_odd:
+            made.start()
+
+    load_gate = w.here(wg_in, wg)
+    load_cot = w.here(cot, ct.at[t])
+    for made in first:
+        made.wait()
+
+    @pl.when(t == z)
+    def _():
+        for made in first_odd:
+            made.wait()
+
+    line_u = LineGather(
+        w, [(lambda b, q: wu.at[:, q, :, cols(b, 256)], False), (lambda b, q: wu.at[:, q, :, odd], True)]
+    )
+    line_d = LineGather(
+        w, [(lambda b, q: wd.at[:, q, :, cols(b, 256)], False), (lambda b, q: wd.at[:, q, :, odd], True)]
+    )
+    line_u.first()
+
+    @pl.loop(0, 16)
+    def _(i):
+        v = x1_ref[rows16(i), :]
+        n2[t, rows16(i), :] = (v * norm_rows(v) * gain_ref[...]).astype(bf16)
+
+    gather = PlaneGather(w, n2)
+    gather.start()
+    load_gate.wait()
+
+    def gate_rows(j):
+        gate[j] = mm(n2[j], wg[...].reshape(1536, 1152))
+
+    gate_rows(t)
+    line_u.step(2)
+    load_cot.wait()
+    gather.forward()
+    gather_cot = PlaneGather(w, ct)
+    gather_cot.start()
+    line_u.step(3)
+    line_d.first()
+    gate_rows(p.tx)
+    gate_rows(p.ty)
+    gather.finish()
+    gate_rows(p.td)
+    line_u.step(4)
+    line_u.finish()
+
+    @pl.loop(0, 4)
+    def _(j):
+        up[j] = mm(n2[j], wu[...].reshape(1536, 1152))
+
+        @pl.loop(0, 16)
+        def _(i):
+            at = rows16(i)
+            value, slope = gelu_pair(gate[j, at, :])
+            u = up[j, at, :]
+            hid[j, at, :] = (value * u).astype(bf16)
+            gate[j, at, :] = value
+            up[j, at, :] = u * slope
+
+    line_d.step(2)
+    gather_cot.forward()
+    line_d.step(3)
+    gather_cot.finish()
+
+    def weight_grad(left, right, out):
+        @pl.loop(0, 4)
+        def _(i):
+            lanes = cols(i, 384)
+            out[i] = (
+                mm_tn(left[:, :, lanes].reshape(1024, 384), right[...].reshape(1024, 1152))
+                .astype(bf16)
+                .reshape(2, 192, 1152)
+            )
+
+    weight_grad(ct, hid, gdown)
+    core_d = CoreSum(w, lambda q: gdown.at[:, q], cb.at[0])
+    core_d.start()
+    line_d.step(4)
+    line_d.finish()
+
+    def grads_rows(j):
+        dh = mm(ct[j], wd[...].reshape(1536, 1152))
+        dga[j] = (dh * up[j]).astype(bf16)
+        dup[j] = (dh * gate[j]).astype(bf16)
+
+    def back_rows(j, n):
+        wide = pl.ds(2 * n, 2)
+        return mm_nt(dga[j], wg[wide].reshape(768, 1152)) + mm_nt(dup[j], wu[wide].reshape(768, 1152))
+
+    def back(j):
+        grads_rows(j)
+        for n in range(2):
+            part[j, :, n * 768 : (n + 1) * 768] = back_rows(j, n).astype(bf16)
+
+    summed = PlaneSum(w, part, far, near)
+    back(p.td)
+    summed.diagonal()
+    core_d.finish()
+    line_sum = LineSum(
+        w,
+        [
+            (lambda j: gdown.at[:, c, :, cols(j, 256)], lambda s, k: landing.at[s * 3 + k - 1], False),
+            (lambda j: gdown.at[:, c, :, odd], lambda s, k: landing_odd.at[s], True),
+        ],
+    )
+    line_sum.first()
+    back(p.ty)
+    summed.to_y()
+    back(p.tx)
+    summed.to_x()
+    line_sum.step(2)
+    grads_rows(t)
+    for n in range(2):
+        own[:, n * 768 : (n + 1) * 768] = back_rows(t, n)
+    line_u.drain()
+    line_d.drain()
+    gather_cot.drain()
+
+    def mid(j):
+        for n in range(2):
+            ct[j, :, n * 768 : (n + 1) * 768] = mm_nt(
+                hid[j], wd[2 * n : 2 * n + 2].reshape(768, 1152)
+            ).astype(bf16)
+
+    branch = PlaneSum(w, ct, far2, near2)
+    mid(p.td)
+    branch.diagonal()
+    mid(p.ty)
+    branch.to_y()
+    mid(p.tx)
+    branch.to_x()
+    for n in range(2):
+        own2[:, n * 768 : (n + 1) * 768] = mm_nt(hid[t], wd[2 * n : 2 * n + 2].reshape(768, 1152))
+    line_sum.step(3)
+    weight_grad(n2, dga, wg)
+    core_g = CoreSum(w, lambda q: wg.at[:, q], cb.at[1])
+    core_g.start()
+    weight_grad(n2, dup, wu)
+    core_u = CoreSum(w, lambda q: wu.at[:, q], cb.at[2])
+    core_u.start()
+    core_g.finish()
+    kept = [w.here(wg.at[:, c], half_out.at[0])]
+    line_sum.step(4)
+    down = Spread(
+        w, [lambda q: gdown.at[q, c, :, cols(z, 256)]], [lambda q: gd_out.at[:, cols(q, 256)]]
+    )
+    down_odd = OddScatter(w, lambda q: gdown.at[q, c, :, odd], gd_out.at[:, odd])
+    summed.finish()
+
+    def dx(i, carry):
+        at = rows16(i)
+        v = x1_ref[at, :]
+        s = norm_rows(v)
+        dn = own[at, :] + near[0, at, :].astype(f32) + near[1, at, :].astype(f32)
+        q = gain_ref[...] * dn
+        dx1_ref[at, :] = (
+            ct[t, at, :].astype(f32) + s * q - v * (s * s * s * jnp.mean(q * v, axis=1, keepdims=True))
+        )
+        g2 = dn * v * s
+        return carry + g2[0:8] + g2[8:16]
+
+    zw = jnp.zeros((8, 1536), f32)
+    g2 = lax.fori_loop(0, 16, dx, zw)
+    core_u.finish()
+    kept.append(w.here(wu.at[:, c], half_out.at[1]))
+    down.start()
+    down_odd.start()
+    branch.finish()
+
+    def last(i, carry):
+        at = rows16(i)
+        m = own2[at, :] + near2[0, at, :].astype(f32) + near2[1, at, :].astype(f32)
+        y = x1_ref[at, :] + m
+        y_ref[at, :] = y.astype(bf16)
+        m2, y2 = m * m, y * y
+        return carry[0] + m2[0:8] + m2[8:16], carry[1] + y2[0:8] + y2[8:16]
+
+    m2, y2 = lax.fori_loop(0, 16, last, (zw, zw))
+    stat_ref[...] = zw
+    stat_ref[2:3, :] = jnp.sum(m2, axis=0, keepdims=True)
+    stat_ref[3:4, :] = jnp.sum(y2, axis=0, keepdims=True)
+    stat_ref[4:5, :] = jnp.sum(g2, axis=0, keepdims=True)
+    down.wait()
+    down_odd.finish()
+    down.drain()
+    for made in kept:
+        made.wait()
+    gather.drain()
+    summed.drain()
+    branch.drain()
+    line_sum.drain()
+    core_d.drain()
+    core_g.drain()
+    core_u.drain()
+
+
+def recurrence_backward(
+    x_ref, gain_ref, dx1_ref, sm_ref, stat1, stat2,
+    win_in, wout_in, n1_in, xb_in, zy_in, zx_in, za_in, c_in, a_in, h_in, o_in, gg_in, half_in,
+    gi_ref, v1_ref, v2_ref, gin_out, gout_out, gff_out, ggate_out,
+    win, wout, n1, dr, xb, zy, zx, za, cc, aa, hh, oo, gg, hgu, tmp, bc, dzy, dzx, dza,
+    part, far, near, own, gin, gout, ggr, cbi, cbo, cbg, land_i, land_o, land_g, land_f, land_fo,
+    tail, sums, gnext, acc8, v1, v2, v1c, v2c, v1z, v2z, send, recv, local,
+):
+    p = Place()
+    w = Wires(p, send, recv, local)
+    t, c, z = p.t, p.c, p.z
+    p.enter()
+    odd = pl.ds(1024, 128)
+
+    load_half = w.here(half_in, hgu)
+    load_out = w.here(wout_in, wout)
+    early = [w.here(a, b) for a, b in ((zy_in, zy), (h_in, hh), (a_in, aa))]
+    later = [
+        w.here(a, b)
+        for a, b in (
+            (zx_in, zx), (za_in, za), (c_in, cc), (gg_in, gg), (o_in, oo), (xb_in, xb), (n1_in, n1), (win_in, win),
+        )
+    ]
+
+    @pl.loop(0, 16)
+    def _(i):
+        dr[t, rows16(i), :] = dx1_ref[rows16(i), :].astype(bf16)
+
+    gather = PlaneGather(w, dr)
+    gather.start()
+    line_f = LineSum(
+        w,
+        [
+            (lambda j: hgu.at[:, :, :, cols(j, 256)], lambda s, k: land_f.at[s * 3 + k - 1], False),
+            (lambda j: hgu.at[:, :, :, odd], lambda s, k: land_fo.at[s], True),
+        ],
+    )
+    load_half.wait()
+    line_f.first()
+    load_out.wait()
+    for made in early:
+        made.wait()
+
+    row = lax.broadcasted_iota(jnp.int32, (8, 512), 0)
+    zero = jnp.zeros((8, 512), f32)
+
+    def scan_rows(j):
+        tmp[...] = mm(dr[j], wout[...].reshape(1536, 512))
+
+        def step(k, carry):
+            i = 15 - k
+            state, product = carry
+            at = rows16(i)
+            value, slope = gelu_pair(zy[j, at, :])
+            do = tmp[at, :]
+            h = hh[j, pl.ds(pl.multiple_of(i * 16 + 8, 8), 16), :]
+            dzy[j, at, :] = (do * h * slope).astype(bf16)
+            flow = do * value
+            follow = aa[j, rows16(i, 24), :][1:17]
+            for half in (8, 0):
+                uv, dv = flow[half : half + 8], follow[half : half + 8]
+                for st in (1, 2, 4):
+                    ok = row < 8 - st
+                    uv = uv + jnp.where(ok, dv * pltpu.roll(uv, 8 - st, 0), 0.0)
+                    dv = jnp.where(ok, dv * pltpu.roll(dv, 8 - st, 0), dv)
+                gv, pv = uv + dv * state, dv * product
+                here = pl.ds(pl.multiple_of(i * 16 + half, 8), 8)
+                zy[j, here, :] = gv
+                bc[j, here, :] = pv
+                state = jnp.broadcast_to(gv[0:1, :], (8, 512))
+                product = jnp.broadcast_to(pv[0:1, :], (8, 512))
+            return state, product
+
+        state, product = lax.fori_loop(0, 16, step, (zero, zero + 1.0))
+        tail[j, 0:8, :] = state
+        tail[j, 8:16, :] = product
+
+    scan_rows(t)
+    gather.forward()
+    scan_rows(p.tx)
+    scan_rows(p.ty)
+    gather.finish()
+    scan_rows(p.td)
+    line_f.step(2)
+
+    base = [w.slot() for _ in range(3)]
+    for away in (1, 2, 3):
+
+        @pl.when(z >= away)
+        def _():
+            w.copy(tail, sums.at[z], base[away - 1], p.line(z - away)).start()
+
+    for made in later:
+        made.wait()
+
+    def out_grad():
+        @pl.loop(0, 4)
+        def _(i):
+            gout[i] = (
+                mm_tn(dr[:, :, cols(i, 384)].reshape(1024, 384), oo[...].reshape(1024, 512))
+                .astype(bf16)
+                .reshape(2, 192, 512)
+            )
+
+    out_grad()
+    core_o = CoreSum(w, lambda q: gout.at[:, q], cbo)
+    core_o.start()
+
+    gnext[...] = jnp.zeros((4, 8, 512), f32)
+    for away in (1, 2, 3):
+
+        @pl.when(z + away <= 3)
+        def _():
+            w.landed(sums.at[z + away], base[away - 1])
+
+    for src in (3, 2, 1):
+
+        @pl.when(z < src)
+        def _():
+            gnext[...] = sums[src, :, 0:8, :] + sums[src, :, 8:16, :] * gnext[...]
+
+    def through(j, carry):
+        after = jnp.concatenate([gnext[j], gnext[j]], axis=0)
+
+        def step(i, carry):
+            sum_x, sum_a, sum_d = carry
+            at = rows16(i)
+            g = zy[j, at, :] + bc[j, at, :] * after
+            before = hh[j, rows16(i, 24), :][7:23]
+            pre_x, pre_a, value = zx[j, at, :], za[j, at, :], cc[j, at, :].astype(f32)
+            rate = jax.nn.sigmoid(pre_a)
+            entry = jax.nn.sigmoid(pre_x)
+            log_a = -8.0 * rate * sm_ref[7:8, :]
+            decay = aa[j, at, :]
+            index = lax.broadcasted_iota(jnp.int32, (16, 512), 0) + i * 16 + z * 256
+            start = index == 0
+            mult = jnp.where(start, 1.0, jnp.sqrt(neg_expm1(2.0 * log_a)))
+            gm = g * mult
+            d_entry = gm * value
+            bc[j, at, :] = gm * entry
+            low_x = (d_entry * entry * (1.0 - entry)).astype(bf16)
+            dzx[j, at, :] = low_x
+            d_mult = g * entry * value
+            d_log = g * before * decay - jnp.where(start, 0.0, d_mult * decay * decay / mult)
+            low_a = (d_log * (-8.0 * sm_ref[7:8, :]) * rate * (1.0 - rate)).astype(bf16)
+            dza[j, at, :] = low_a
+            wide_x, wide_a, d_decay = low_x.astype(f32), low_a.astype(f32), d_log * rate
+            return (
+                sum_x + wide_x[0:8] + wide_x[8:16],
+                sum_a + wide_a[0:8] + wide_a[8:16],
+                sum_d + d_decay[0:8] + d_decay[8:16],
+            )
+
+        carry = lax.fori_loop(0, 16, step, carry)
+        for b in range(4):
+            lanes = pl.ds(b * 128, 128)
+            bc[j, pl.ds(0, 256), lanes] += mm_nt(
+                dzx[j, :, lanes], gg[0, b].reshape(128, 128)
+            ) + mm_nt(dza[j, :, lanes], gg[1, b].reshape(128, 128))
+        return carry
+
+    sum_x, sum_a, sum_d = lax.fori_loop(0, 4, through, (zero, zero, zero))
+    acc8[5:6, :] = jnp.sum(sum_x, axis=0, keepdims=True)
+    acc8[6:7, :] = jnp.sum(sum_a, axis=0, keepdims=True)
+    acc8[7:8, :] = -8.0 * sm_ref[8:9, :] * jnp.sum(sum_d, axis=0, keepdims=True)
+
+    halo = w.slot()
+
+    @pl.when(z > 0)
+    def _():
+        w.copy(bc.at[:, pl.ds(0, 8)], bc.at[:, pl.ds(256, 8)], halo, p.line(z - 1)).start()
+
+    @pl.when(z == 3)
+    def _():
+        bc[:, 256:264, :] = jnp.zeros((4, 8, 512), f32)
+
+    line_f.step(3)
+    core_o.finish()
+    line_o = LineSum(w, [(lambda j: gout.at[:, c, :, cols(j)], lambda s, k: land_o.at[s * 3 + k - 1], False)])
+
+    for b in range(4):
+        lanes = pl.ds(b * 128, 128)
+        left = cc[:, :, lanes].reshape(1024, 128)
+        for i, right in ((0, dzx), (1, dza)):
+            ggr[i, b] = (
+                mm_tn(left, right[:, :, lanes].reshape(1024, 128)).astype(bf16).reshape(4, 2, 16, 128)
+            )
+
+    @pl.when(z < 3)
+    def _():
+        w.landed(bc.at[:, pl.ds(256, 8)], halo)
+
+    def taps(j, carry):
+        def step(i, carry):
+            at = rows16(i)
+            v = bc[j, rows16(i, 24), :]
+            xv = xb[j, rows16(i, 24), :]
+            total = sm_ref[0:1, :] * v[0:16]
+            for k in (1, 2, 3):
+                total = total + sm_ref[k : k + 1, :] * v[k : k + 16]
+            cc[j, at, :] = total.astype(bf16)
+            now = v[0:16]
+            new = []
+            for k in range(4):
+                product = now * xv[8 - k : 24 - k]
+                new.append(carry[k] + product[0:8] + product[8:16])
+            new.append(carry[4] + now[0:8] + now[8:16])
+            return tuple(new)
+
+        return lax.fori_loop(0, 16, step, carry)
+
+    tap_sums = lax.fori_loop(0, 4, taps, (zero,) * 5)
+    for k in range(5):
+        acc8[k : k + 1, :] = jnp.sum(tap_sums[k], axis=0, keepdims=True)
+
+    def back_rows(j, n):
+        wide = pl.ds(2 * n, 2)
+        return mm_nt(cc[j], win[0, wide].reshape(768, 512)) + mm_nt(dzy[j], win[1, wide].reshape(768, 512))
+
+    def back(j):
+        for n in range(2):
+            part[j, :, n * 768 : (n + 1) * 768] = back_rows(j, n).astype(bf16)
+
+    summed = PlaneSum(w, part, far, near)
+    back(p.td)
+    summed.diagonal()
+
+    @pl.loop(0, 4)
+    def _(i):
+        left = n1[:, :, cols(i, 384)].reshape(1024, 384)
+        gin[0, i] = mm_tn(left, cc[...].reshape(1024, 512)).astype(bf16).reshape(2, 192, 512)
+        gin[1, i] = mm_tn(left, dzy[...].reshape(1024, 512)).astype(bf16).reshape(2, 192, 512)
+
+    core_i = CoreSum(w, lambda q: gin.at[:, :, q], cbi)
+    core_i.start()
+    core_g = CoreSum(w, lambda q: ggr.at[:, :, :, q], cbg)
+    core_g.start()
+    back(p.ty)
+    summed.to_y()
+    back(p.tx)
+    summed.to_x()
+    line_f.step(4)
+    line_o.first()
+    send_f = Spread(
+        w,
+        [lambda q: hgu.at[:, q, :, cols(z, 256)]],
+        [lambda q: gff_out.at[:, :, cols(q, 256)]],
+    )
+    send_fo = OddScatter(w, lambda q: hgu.at[:, q, :, odd], gff_out.at[:, :, odd])
+    core_i.finish()
+    core_g.finish()
+    line_i = LineSum(
+        w,
+        [
+            (lambda j: gin.at[:, :, c, :, cols(j)], lambda s, k: land_i.at[s * 3 + k - 1], False),
+            (lambda j: ggr.at[:, j, :, c], lambda s, k: land_g.at[s * 3 + k - 1], False),
+        ],
+    )
+    line_i.first()
+    for n in range(2):
+        own[:, n * 768 : (n + 1) * 768] = back_rows(t, n)
+    line_o.step(2)
+    line_i.step(2)
+    line_o.step(3)
+    line_i.step(3)
+    summed.finish()
+    send_f.start()
+    send_fo.start()
+
+    def last(i, carry):
+        at = rows16(i)
+        v = x_ref[at, :].astype(f32)
+        s = norm_rows(v)
+        dn = own[at, :] + near[0, at, :].astype(f32) + near[1, at, :].astype(f32)
+        q = gain_ref[...] * dn
+        gi_ref[at, :] = (
+            dx1_ref[at, :] + s * q - v * (s * s * s * jnp.mean(q * v, axis=1, keepdims=True))
+        ).astype(bf16)
+        g1 = dn * v * s
+        return carry + g1[0:8] + g1[8:16]
+
+    g1 = lax.fori_loop(0, 16, last, jnp.zeros((8, 1536), f32))
+    v1[0] = stat1[...] + stat2[...]
+    v1[0, 5:6, :] = jnp.sum(g1, axis=0, keepdims=True)
+    v2[0] = jnp.zeros((32, 512), f32)
+    v2[0, pl.ds(pl.multiple_of(t * 8, 8), 8), :] = acc8[...]
+    stage_slots = [(w.slot(), w.slot()) for _ in range(3)]
+    for n, device in enumerate((p.partner(), p.plane(p.tx), p.plane(p.ty))):
+        s1, s2 = stage_slots[n]
+        w.copy(v1.at[n], v1c.at[n], s1, device).start()
+        w.copy(v2.at[n], v2c.at[n], s2, device).start()
+        if n == 0:
+            line_o.step(4)
+            send_o = Spread(w, [lambda q: gout.at[q, c, :, cols(z)]], [lambda q: gout_out.at[:, cols(q)]])
+            send_o.start()
+        if n == 1:
+            line_i.step(4)
+            send_i = Spread(
+                w,
+                [lambda q: gin.at[:, q, c, :, cols(z)], lambda q: ggr.at[:, z, q, c]],
+                [lambda q: gin_out.at[:, :, cols(q)], lambda q: ggate_out.at[:, q]],
+            )
+            send_i.start()
+        w.landed(v1c.at[n], s1)
+        w.landed(v2c.at[n], s2)
+        v1[n + 1] = v1[n] + v1c[n]
+        v2[n + 1] = v2[n] + v2c[n]
+    line_slots = [(w.slot(), w.slot()) for _ in range(3)]
+    for k in (1, 2, 3):
+        s1, s2 = line_slots[k - 1]
+        w.copy(v1.at[3], v1z.at[z], s1, p.line(p.around(k))).start()
+        w.copy(v2.at[3], v2z.at[z], s2, p.line(p.around(k))).start()
+    v1z[z] = v1[3]
+    v2z[z] = v2[3]
+    for k in (1, 2, 3):
+        s1, s2 = line_slots[k - 1]
+        w.landed(v1z.at[p.around(4 - k)], s1)
+        w.landed(v2z.at[p.around(4 - k)], s2)
+    v1_ref[...] = v1z[0] + v1z[1] + v1z[2] + v1z[3]
+    v2_ref[...] = v2z[0] + v2z[1] + v2z[2] + v2z[3]
+
+    send_f.wait()
+    send_fo.finish()
+    send_o.wait()
+    send_i.wait()
+    send_f.drain()
+    send_o.drain()
+    send_i.drain()
+    for n in range(3):
+        s1, s2 = stage_slots[n]
+        w.sent(v1.at[n], s1)
+        w.sent(v2.at[n], s2)
+        s1, s2 = line_slots[n]
+        w.sent(v1.at[3], s1)
+        w.sent(v2.at[3], s2)
+    gather.drain()
+    summed.drain()
+    line_f.drain()
+    line_o.drain()
+    line_i.drain()
+    core_o.drain()
+    core_i.drain()
+    core_g.drain()
+
+    for away in (1, 2, 3):
+
+        @pl.when(z >= away)
+        def _():
+            w.sent(tail, base[away - 1])
+
+    @pl.when(z > 0)
+    def _():
+        w.sent(bc.at[:, pl.ds(0, 8)], halo)
+
+
+def forward_backward_ff(x1, g2, cot, wg, a2u, a2d):
+    V = pltpu.VMEM
+    outs = [
+        shape((256, 1536), f32), shape((256, 1536), bf16), shape((8, 1536), f32),
+        shape((2, 4, 192, 1152), bf16), shape((192, 1152), bf16),
+    ]
+    weights = V((4, 2, 192, 1152), bf16)
+    tokens = V((4, 256, 1536), bf16)
+    hidden, hidden_low = V((4, 256, 1152), f32), V((4, 256, 1152), bf16)
+    far, near, own = V((2, 128, 1536), bf16), V((2, 256, 1536), bf16), V((256, 1536), f32)
+    scratch = [
+        weights, weights, weights, tokens, tokens, hidden, hidden, hidden_low, hidden_low, hidden_low,
+        tokens, far, near, far, near, own, own, weights, V((3, 4, 192, 1152), bf16),
+        V((6, 4, 192, 256), bf16), V((2, 4, 192, 128), bf16),
+    ]
+    return call(
+        feed_forward, 1, (x1, g2, cot, wg, a2u, a2d), "vvaaaa", outs, "vvvaa", scratch, 128, 24, "feed_forward"
+    )
+
+
+def backward_recurrence(x, g1, dx1, sm, stat1, stat2, *saved):
+    V = pltpu.VMEM
+    outs = [
+        shape((256, 1536), bf16), shape((8, 1536), f32), shape((32, 512), f32),
+        shape((2, 192, 512), bf16), shape((192, 512), bf16), shape((2, 192, 1152), bf16), shape((2, 4, 16, 128), bf16),
+    ]
+    tokens = V((4, 256, 1536), bf16)
+    wide, padded, low = V((4, 256, 512), f32), V((4, 264, 512), f32), V((4, 256, 512), bf16)
+    scratch = [
+        V((2, 4, 2, 192, 512), bf16), V((4, 2, 192, 512), bf16), tokens, tokens, padded, wide, wide, wide, low,
+        padded, padded, low, V((2, 4, 4, 2, 16, 128), bf16), V((2, 4, 192, 1152), bf16), V((256, 512), f32),
+        padded, low, low, low,
+        tokens, V((2, 128, 1536), bf16), V((2, 256, 1536), bf16), V((256, 1536), f32),
+        V((2, 4, 2, 192, 512), bf16), V((4, 2, 192, 512), bf16), V((2, 4, 4, 2, 16, 128), bf16),
+        V((2, 4, 192, 512), bf16), V((4, 192, 512), bf16), V((2, 4, 4, 16, 128), bf16),
+        V((6, 2, 4, 192, 128), bf16), V((6, 4, 192, 128), bf16), V((6, 2, 4, 16, 128), bf16),
+        V((6, 2, 4, 192, 256), bf16), V((2, 2, 4, 192, 128), bf16),
+        V((4, 16, 512), f32), V((4, 4, 16, 512), f32), V((4, 8, 512), f32), V((8, 512), f32),
+        V((4, 8, 1536), f32), V((4, 32, 512), f32), V((3, 8, 1536), f32), V((3, 32, 512), f32),
+        V((4, 8, 1536), f32), V((4, 32, 512), f32),
+    ]
+    return call(
+        recurrence_backward, 2, (x, g1, dx1, sm, stat1, stat2) + saved, "vvvvvv" + "a" * 13,
+        outs, "vvvaaaa", scratch, 160, 24, "recurrence_backward",
+    )
+
+
+def fast_local(
+    inputs, norm1_gain, w_in_x, w_in_y, conv_w, conv_b, gates, gate_bias, decay_param, w_out,
+    norm2_gain, w_gate, w_up, w_down, cotangent,
+):
+    channels = conv_b.shape[0]
+    small = jnp.concatenate(
+        [
+            conv_w, conv_b[None], gate_bias, jax.nn.softplus(decay_param)[None],
+            jax.nn.sigmoid(decay_param)[None], jnp.zeros((7, channels), f32),
+        ],
+        axis=0,
+    )
+    g1, g2 = norm1_gain[None], norm2_gain[None]
+    (x1, stat1, sm, n1, win, wout, wg, a2u, a2d, gg, xb, zy, zx, za, cc, aa, hh, oo) = forward_recurrence(
+        inputs, g1, small, w_in_x, w_in_y, w_out, gates, w_gate, w_up, w_down
+    )
+    dx1, output, stat2, halves, gd = forward_backward_ff(x1, g2, cotangent, wg, a2u, a2d)
+    gi, v1, v2, gin, gout, gff, ggate = backward_recurrence(
+        inputs, g1, dx1, sm, stat1, stat2, win, wout, n1, xb, zy, zx, za, cc, aa, hh, oo, gg, halves
+    )
+    squares = jnp.sum(v1[0:4], axis=1)
+    count = inputs.shape[0] * lax.axis_size("dp") * lax.axis_size("tensor") * inputs.shape[1]
+    stream_rms = jnp.sqrt(squares / count)
+    rows = v2.reshape(4, 8, 4, 128).transpose(1, 2, 0, 3).reshape(8, 4 * channels)
+    return (
+        output, gi, v1[5], gin[0].astype(f32), gin[1].astype(f32), rows[0:4], rows[4], ggate.astype(f32),
+        rows[5:7], rows[7], gout.astype(f32), v1[4], gff[0].astype(f32), gff[1].astype(f32), gd.astype(f32),
+        stream_rms,
+    )
+
+
 def solution(mesh):
+    fits = mesh.shape["dp"] == 8 and mesh.shape["tensor"] == 4
     return jax.shard_map(
-        local,
+        fast_local if fits else local,
         mesh=mesh,
         in_specs=(
             P(("dp", "tensor"), None),

time: 1950 us -> 454 us (0.23); the launches traced: 1920 us -> 445 us
  waiting for transfers between devices: 1120 us -> 0 us
  local copies, waits for them, and re-layouts: 442 us -> 10.6 us
  Pallas kernels: 0 us -> 424 us
  other arithmetic: 150 us -> 9.62 us
  matrix products: 138 us -> 0 us
  blocking collectives: 51.8 us -> 0 us
    reduce_scatter x10 -> x0, waiting for transfers between devices: 713 us -> none  [the longest x1 113 us: local(): lax.psum_scatter(back_product(hidden, mlp_d), 'tensor', scatter_dimension...]
    pallas_call x0 -> x3, Pallas kernels: none -> 424 us  [call(): pl.pallas_call(kernel, out_shape=outs, in_specs=[kinds[k] for k in spaces...]
    all_gather x10 -> x0, waiting for transfers between devices: 295 us -> none  [the longest x1 65.8 us: local(): full_two = lax.all_gather(n_two, 'tensor', axis=0, tiled=True)]
    slice x131 -> x6, local copies, waits for them, and re-layouts: 290 us -> 3.39 us  [the longest x1 1.51 us: fast_local(): v1[4]]
    dot_general x24 -> x0, matrix products: 138 us -> none  [the longest x6 44.5 us: row_product(): lax.dot_general(left, right, (((0,), (0,)), ((), ())), preferred_element_...]
    unnamed x23 -> x0, waiting for transfers between devices: 74 us -> none
    pad x36 -> x0, local copies, waits for them, and re-layouts: 71.9 us -> none  [the longest x18 36 us: local(): lax.associative_scan(combine, (next_decay, d_states.reshape(seq_count, SE...]
    psum x1 -> x0, blocking collectives: 42.1 us -> none  [local(): lax.psum((jnp.stack([grad_gain_one, grad_gain_two]), spread_grads, square...]
  transfers between devices with their start and end apart: 22 -> 0, of which waited for: 20 -> 0; matrix products, arithmetic and copies ran while one was open for 21% -> 0% of each run, Pallas kernels for 0% -> 0%
where the time goes in v1:
time: 454 us; the launch traced here: 445 us
  Pallas kernels  424 us (93%)
  local copies, waits for them, and re-layouts  10.6 us (2%)
  other arithmetic  9.62 us (2%)
    pallas_call x3, Pallas kernels, call(): pl.pallas_call(kernel, out_shape=outs, in_specs=[kinds[k] for k in spaces...  424 us

profile of v1, /device:TPU:4, one launch (start us, length us, event | category | flops | bytes accessed | tf_op | source)
XLA Modules:
  0.0 445.1 jit_solution(16556007446535542477)
XLA Ops:
  0.6 0.7 add_divide_fusion
  1.3 1.3 broadcast_in_dim.18.gain_ref
  2.6 1.3 broadcast_in_dim.23.gain_ref
  3.9 2.0 concatenate.3.small_ref
  5.9 108.3 %recurrence_forward.1 = (f32[256,1536]{1,0:T(8,128)}, f32[8,1536]{1,0:T(8,128)}, f32[16,512]{1,0:T(8,128)}, bf16[4,256,1536]{2,1,0:T(8,128)(2,1)}, bf16[2,4,2,19...) custom-call(bf16[256,1536]{1,0:T(8,128)(2,1)} %x_ref.3, ...), custom_call_target="tpu_custom_call" | custom-call | tf_op jit(solution)/shard_map/recurrence_forward/pallas_call | solution.py:997
  114.2 156.2 %feed_forward.1 = (f32[256,1536]{1,0:T(8,128)}, bf16[256,1536]{1,0:T(8,128)(2,1)}, f32[8,1536]{1,0:T(8,128)}, bf16[2,4,192,1152]{3,2,1,0:T(8,128)(2,1)}, bf16[192,1152]{1,0:T(8,128)(2,1)}) custom-call(f32[256,1536]{1,0:T(8,128)} %get-tuple-element.46.x1_ref, f32[1,1536]{1,0:T(1,128)} %broadcast_in_dim.23.gain_ref, bf16[256,1536]{1,0:T(8,128)(2,1)} %cot.1, ...), custom_call_target="tpu_custom_call" | custom-call | tf_op jit(solution)/shard_map/feed_forward/pallas_call | solution.py:997
  270.4 159.2 %recurrence_backward.1 = (bf16[256,1536]{1,0:T(8,128)(2,1)}, f32[8,1536]{1,0:T(8,128)}, f32[32,512]{1,0:T(8,128)}, bf16[2,192,512]{2,1,0:T(8,128)(2,1)}, bf16[19...) custom-call(bf16[256,1536]{1,0:T(8,128)(2,1)} %x_ref.3, ...), custom_call_target="tpu_custom_call" | custom-call | tf_op jit(solution)/shard_map/recurrence_backward/pallas_call | solution.py:997
  429.6 0.0 copy-start.3
  429.6 0.0 copy-start
  429.6 1.0 slice_reduce_fusion
  430.7 1.5 slice_reduce_fusion.1
  432.2 0.5 multiply_sqrt_fusion
  432.7 0.9 copy.35
  433.6 0.6 slice.48
  434.2 0.6 fusion
  434.8 0.6 slice.45
  435.5 1.4 convert_element_type.37
  436.8 1.7 convert_element_type.38
  438.6 2.0 bitcast_convert_fusion.2
  440.6 0.0 copy-start.1
  440.6 0.0 copy-done.3
  440.6 1.0 convert_element_type.43
  441.5 0.0 copy-done
  441.5 0.0 copy-start.2
  441.5 1.3 bitcast_convert_fusion
  442.9 0.0 copy-done.1
  442.9 0.9 copy.38
  443.7 0.0 copy-done.2
  443.7 0.9 copy.39
  (3 shorter events, 0.0 us)
Async XLA Ops:
  429.6 11.0 %copy-start.3 = (bf16[192,1152]{1,0:T(8,128)(2,1)S(1)}, bf16[192,1152]{1,0:T(8,128)(2,1)}, u32[]{:S(2)}) copy-start(bf16[192,1152]{1,0:T(8,128)(2,1)} %get-tuple-element.75) | copy-start | bytes 1327108
  429.6 11.9 %copy-start = (bf16[2,192,1152]{2,1,0:T(8,128)(2,1)S(1)}, bf16[2,192,1152]{2,1,0:T(8,128)(2,1)}, u32[]{:S(2)}) copy-start(bf16[2,192,1152]{2,1,0:T(8,128)(2,1)} %get-tuple-element.74) | copy-start | bytes 2654212
  440.6 2.3 copy-start.1
  441.5 2.2 copy-start.2

commit v2 on v1

v2 whole, which is shorter than its diff:
```python
import functools

import jax
import jax.numpy as jnp
from jax import lax
from jax.experimental import pallas as pl
from jax.experimental.pallas import tpu as pltpu
from jax.sharding import PartitionSpec as P

CONV = 4
SEQ_LEN = 1024


epsilon = 1e-06


def gelu_tanh(value):
    return jax.nn.gelu(value, approximate=True)


def combine(earlier, later):
    return (earlier[0] * later[0], later[0] * earlier[1] + later[1])


def norm_back(value, scale, gain, grad):
    scaled = gain * grad
    return scale * scaled - value * scale * scale * scale * jnp.mean(
        scaled * value, axis=1, keepdims=True
    )


def row_product(left, right):
    return lax.dot_general(
        left, right, (((0,), (0,)), ((), ())), preferred_element_type=jnp.float32
    )


def back_product(left, right):
    return lax.dot_general(
        left, right, (((1,), (1,)), ((), ())), preferred_element_type=jnp.float32
    )


def local(
    inputs,
    norm1_gain,
    w_in_x,
    w_in_y,
    conv_w,
    conv_b,
    gates,
    gate_bias,
    decay_param,
    w_out,
    norm2_gain,
    w_gate,
    w_up,
    w_down,
    cotangent,
):
    row_count = inputs.shape[0]
    model_width = inputs.shape[1]
    tensor_count = lax.axis_size("tensor")
    group_rows = row_count * tensor_count
    seq_count = group_rows // SEQ_LEN
    rec_x, rec_y, rec_o, gate_mats = (
        lax.all_gather(w_in_x, "dp", axis=0, tiled=True),
        lax.all_gather(w_in_y, "dp", axis=0, tiled=True),
        lax.all_gather(w_out, "dp", axis=0, tiled=True),
        lax.all_gather(gates, "dp", axis=2, tiled=True),
    )
    channels = rec_x.shape[1]
    blocks_here = gate_mats.shape[1]
    block_width = gate_mats.shape[3]
    residual = inputs.astype(jnp.float32)
    scale_one = lax.rsqrt(jnp.mean(residual * residual, axis=1, keepdims=True) + epsilon)
    n_one = (residual * scale_one * norm1_gain).astype(jnp.bfloat16)
    full_one = lax.all_gather(n_one, "tensor", axis=0, tiled=True)
    x_branch = jnp.dot(full_one, rec_x, preferred_element_type=jnp.float32)
    y_pre = jnp.dot(full_one, rec_y, preferred_element_type=jnp.float32)
    seq_x = x_branch.reshape(seq_count, SEQ_LEN, channels)
    padded = jnp.pad(seq_x, ((0, 0), (CONV - 1, 0), (0, 0)))
    conv_sum = conv_b + jnp.zeros_like(seq_x)
    for k in range(CONV):
        conv_sum = conv_sum + conv_w[k] * padded[:, CONV - 1 - k : CONV - 1 - k + SEQ_LEN]
    conv_low = conv_sum.reshape(group_rows, channels).astype(jnp.bfloat16)
    conv_value = conv_low.astype(jnp.float32)
    blocked = conv_low.reshape(group_rows, blocks_here, block_width)
    z_input = (
        jnp.einsum(
            "gbi,bij->gbj", blocked, gate_mats[0], preferred_element_type=jnp.float32
        ).reshape(group_rows, channels)
        + gate_bias[0]
    )
    z_decay = (
        jnp.einsum(
            "gbi,bij->gbj", blocked, gate_mats[1], preferred_element_type=jnp.float32
        ).reshape(group_rows, channels)
        + gate_bias[1]
    )
    seq_start = (jnp.arange(group_rows) % SEQ_LEN == 0)[:, None]

    def coefficients(input_pre, decay_pre, conv_part, decay_raw):
        log_decay = -8.0 * jax.nn.sigmoid(decay_pre) * jax.nn.softplus(decay_raw)
        mult = jnp.where(seq_start, 1.0, jnp.sqrt(-jnp.expm1(2.0 * log_decay)))
        return (jnp.exp(log_decay), mult * jax.nn.sigmoid(input_pre) * conv_part)

    (decays, inflow), pull_coeff = jax.vjp(coefficients, z_input, z_decay, conv_value, decay_param)
    seq_decay = decays.reshape(seq_count, SEQ_LEN, channels)
    _, seq_states = lax.associative_scan(
        combine, (seq_decay, inflow.reshape(seq_count, SEQ_LEN, channels)), axis=1
    )
    states = seq_states.reshape(group_rows, channels)
    y_gate = gelu_tanh(y_pre)
    mixed_out = (states * y_gate).astype(jnp.bfloat16)
    branch = lax.psum_scatter(
        back_product(mixed_out, rec_o), "tensor", scatter_dimension=0, tiled=True
    )
    stream = residual + branch
    mlp_g, mlp_u, mlp_d = (
        lax.all_gather(w_gate, "dp", axis=0, tiled=True),
        lax.all_gather(w_up, "dp", axis=0, tiled=True),
        lax.all_gather(w_down, "dp", axis=0, tiled=True),
    )
    scale_two = lax.rsqrt(jnp.mean(stream * stream, axis=1, keepdims=True) + epsilon)
    n_two = (stream * scale_two * norm2_gain).astype(jnp.bfloat16)
    full_two = lax.all_gather(n_two, "tensor", axis=0, tiled=True)
    gate_pre = jnp.dot(full_two, mlp_g, preferred_element_type=jnp.float32)
    up_pre = jnp.dot(full_two, mlp_u, preferred_element_type=jnp.float32)
    hidden = (gelu_tanh(gate_pre) * up_pre).astype(jnp.bfloat16)
    ffn_out = lax.psum_scatter(
        back_product(hidden, mlp_d), "tensor", scatter_dimension=0, tiled=True
    )
    result = stream + ffn_out
    output = result.astype(jnp.bfloat16)
    squares = jnp.stack(
        [
            jnp.sum(stream * stream),
            jnp.sum(branch * branch),
            jnp.sum(ffn_out * ffn_out),
            jnp.sum(result * result),
        ]
    )
    upstream = cotangent.astype(jnp.float32)
    full_cot = lax.all_gather(cotangent, "tensor", axis=0, tiled=True)
    d_hidden = jnp.dot(full_cot, mlp_d, preferred_element_type=jnp.float32)
    grad_down = row_product(full_cot, hidden)
    _, pull_mlp = jax.vjp(
        lambda gate_value, up_value: gelu_tanh(gate_value) * up_value, gate_pre, up_pre
    )
    d_gate, d_up = pull_mlp(d_hidden)
    d_gate_low = d_gate.astype(jnp.bfloat16)
    d_up_low = d_up.astype(jnp.bfloat16)
    grad_gate_w = row_product(full_two, d_gate_low)
    grad_up_w = row_product(full_two, d_up_low)
    d_two = lax.psum_scatter(
        back_product(d_gate_low, mlp_g) + back_product(d_up_low, mlp_u),
        "tensor",
        scatter_dimension=0,
        tiled=True,
    )
    grad_gain_two = jnp.sum(d_two * stream * scale_two, axis=0)
    d_stream = upstream + norm_back(stream, scale_two, norm2_gain, d_two)
    mlp_summed = (grad_gate_w, grad_up_w, grad_down)
    full_branch = lax.all_gather(d_stream.astype(jnp.bfloat16), "tensor", axis=0, tiled=True)
    d_mixed = jnp.dot(full_branch, rec_o, preferred_element_type=jnp.float32)
    grad_out_w = row_product(full_branch, mixed_out)
    d_states = d_mixed * y_gate
    _, pull_gelu = jax.vjp(gelu_tanh, y_pre)
    d_y_low = pull_gelu(d_mixed * states)[0].astype(jnp.bfloat16)
    next_decay = jnp.concatenate([seq_decay[:, 1:], jnp.zeros_like(seq_decay[:, :1])], axis=1)
    _, carried = lax.associative_scan(
        combine, (next_decay, d_states.reshape(seq_count, SEQ_LEN, channels)), reverse=True, axis=1
    )
    prev_states = jnp.concatenate([jnp.zeros_like(seq_states[:, :1]), seq_states[:, :-1]], axis=1)
    d_decays = (carried * prev_states).reshape(group_rows, channels)
    d_input_pre, d_decay_pre, d_conv_direct, grad_decay = pull_coeff(
        (d_decays, carried.reshape(group_rows, channels))
    )
    d_input_low = d_input_pre.astype(jnp.bfloat16)
    d_decay_low = d_decay_pre.astype(jnp.bfloat16)
    grad_bias = jnp.stack(
        [
            jnp.sum(d_input_low, axis=0, dtype=jnp.float32),
            jnp.sum(d_decay_low, axis=0, dtype=jnp.float32),
        ]
    )
    input_blocks = d_input_low.reshape(group_rows, blocks_here, block_width)
    decay_blocks = d_decay_low.reshape(group_rows, blocks_here, block_width)
    grad_gate_mats = jnp.stack(
        [
            jnp.einsum("gbi,gbj->bij", blocked, input_blocks, preferred_element_type=jnp.float32),
            jnp.einsum("gbi,gbj->bij", blocked, decay_blocks, preferred_element_type=jnp.float32),
        ]
    )
    d_conv = d_conv_direct + jnp.einsum(
        "gbj,bij->gbi", input_blocks, gate_mats[0], preferred_element_type=jnp.float32
    ).reshape(group_rows, channels)
    d_conv = d_conv + jnp.einsum(
        "gbj,bij->gbi", decay_blocks, gate_mats[1], preferred_element_type=jnp.float32
    ).reshape(group_rows, channels)
    seq_dconv = d_conv.reshape(seq_count, SEQ_LEN, channels)
    grad_conv_b = jnp.sum(seq_dconv, axis=(0, 1))
    padded_back = jnp.pad(seq_dconv, ((0, 0), (0, CONV - 1), (0, 0)))
    tap_grads = []
    d_x_seq = jnp.zeros_like(seq_dconv)
    for k in range(CONV):
        tap_grads.append(
            jnp.sum(seq_dconv * padded[:, CONV - 1 - k : CONV - 1 - k + SEQ_LEN], axis=(0, 1))
        )
        d_x_seq = d_x_seq + conv_w[k] * padded_back[:, k : k + SEQ_LEN]
    grad_conv_w = jnp.stack(tap_grads)
    d_x_low = d_x_seq.reshape(group_rows, channels).astype(jnp.bfloat16)
    grad_in_x_w = row_product(full_one, d_x_low)
    grad_in_y_w = row_product(full_one, d_y_low)
    d_one = lax.psum_scatter(
        back_product(d_x_low, rec_x) + back_product(d_y_low, rec_y),
        "tensor",
        scatter_dimension=0,
        tiled=True,
    )
    grad_gain_one = jnp.sum(d_one * residual * scale_one, axis=0)
    grad_inputs = (d_stream + norm_back(residual, scale_one, norm1_gain, d_one)).astype(
        jnp.bfloat16
    )
    small_grads = jnp.concatenate(
        [grad_conv_w, grad_conv_b[None], grad_bias, grad_decay[None]], axis=0
    )
    spread_grads = lax.dynamic_update_slice(
        jnp.zeros((small_grads.shape[0], channels * tensor_count), jnp.float32),
        small_grads,
        (0, lax.axis_index("tensor") * channels),
    )
    gain_total, small_total, square_total = lax.psum(
        (jnp.stack([grad_gain_one, grad_gain_two]), spread_grads, squares), ("dp", "tensor")
    )
    stream_rms = jnp.sqrt(
        square_total / (row_count * lax.axis_size("dp") * tensor_count * model_width)
    )
    summed_all = (
        lax.psum_scatter(grad_in_x_w, "dp", scatter_dimension=0, tiled=True),
        lax.psum_scatter(grad_in_y_w, "dp", scatter_dimension=0, tiled=True),
        lax.psum_scatter(grad_out_w, "dp", scatter_dimension=0, tiled=True),
        lax.psum_scatter(grad_gate_mats, "dp", scatter_dimension=2, tiled=True),
        lax.psum_scatter(mlp_summed[0], "dp", scatter_dimension=0, tiled=True),
        lax.psum_scatter(mlp_summed[1], "dp", scatter_dimension=0, tiled=True),
        lax.psum_scatter(mlp_summed[2], "dp", scatter_dimension=0, tiled=True),
    )
    rec_summed = summed_all[:4]
    grad_gate_sum, grad_up_sum, grad_down_sum = (summed_all[4], summed_all[5], summed_all[6])
    return (
        output,
        grad_inputs,
        gain_total[0],
        rec_summed[0],
        rec_summed[1],
        small_total[0:CONV],
        small_total[CONV],
        rec_summed[3],
        small_total[CONV + 1 : CONV + 3],
        small_total[CONV + 3],
        rec_summed[2],
        gain_total[1],
        grad_gate_sum,
        grad_up_sum,
        grad_down_sum,
        stream_rms,
    )


MESH = pl.DeviceIdType.MESH
bf16 = jnp.bfloat16
f32 = jnp.float32
VMEM_BYTES = 67043328


def mm(a, b):
    return jnp.dot(a, b, preferred_element_type=f32)


def mm_nt(a, b):
    return lax.dot_general(a, b, (((1,), (1,)), ((), ())), preferred_element_type=f32)


def mm_tn(a, b):
    return lax.dot_general(a, b, (((0,), (0,)), ((), ())), preferred_element_type=f32)


def gelu_value(x):
    return 0.5 * x * (1.0 + jnp.tanh(0.7978845608028654 * x * (1.0 + 0.044715 * (x * x))))


def gelu_pair(x):
    x2 = x * x
    th = jnp.tanh(0.7978845608028654 * x * (1.0 + 0.044715 * x2))
    cdf = 0.5 * (1.0 + th)
    slope = 0.5 * x * (1.0 - th * th) * (0.7978845608028654 * (1.0 + 0.134145 * x2))
    return x * cdf, cdf + slope


def one_minus_square(x, decay):
    series = x * (
        1.0
        + x * (0.5 + x * (1 / 6 + x * (1 / 24 + x * (1 / 120 + x * (1 / 720 + x * (1 / 5040))))))
    )
    return jnp.where(x > -0.35, -series, 1.0 - decay * decay)


class Place:
    def __init__(self):
        self.d = lax.axis_index("dp")
        self.z = lax.axis_index("tensor")
        self.t = lax.div(self.d, 2)
        self.c = lax.rem(self.d, 2)
        self.tx = self.t + 1 - 2 * lax.rem(self.t, 2)
        self.ty = self.t + 2 - 4 * lax.div(self.t, 2)
        self.td = 3 - self.t
        self.peers = (self.tx, self.ty, self.td)

    def member(self, r):
        x, y = lax.rem(self.t, 2), lax.div(self.t, 2)
        b, e = lax.rem(r, 2), lax.div(r, 2)
        return x + b - 2 * x * b + 2 * (y + e - 2 * y * e)

    def plane(self, t):
        return (2 * t + self.c, self.z)

    def line(self, z):
        return (self.d, z)

    def partner(self):
        return (2 * self.t + 1 - self.c, self.z)

    def around(self, k):
        return lax.rem(self.z + k, 4)

    def enter(self):
        barrier = pltpu.get_barrier_semaphore()
        targets = [self.plane(t) for t in self.peers] + [self.partner()]
        targets += [self.line(self.around(k)) for k in (1, 2, 3)]
        for target in targets:
            pl.semaphore_signal(barrier, inc=1, device_id=target, device_id_type=MESH)
        pl.semaphore_wait(barrier, len(targets))


class Wires:
    def __init__(self, place, send, recv, local):
        self.place, self.send, self.recv, self.local = place, send, recv, local
        self.used, self.used_local = 0, 0

    def slot(self):
        self.used += 1
        assert self.used <= self.send.shape[0]
        return self.used - 1

    def block(self, count):
        self.used += count
        assert self.used <= self.send.shape[0]
        return self.used - count

    def copy(self, src, dst, slot, device):
        return pltpu.make_async_remote_copy(
            src_ref=src,
            dst_ref=dst,
            send_sem=self.send.at[slot],
            recv_sem=self.recv.at[slot],
            device_id=device,
            device_id_type=MESH,
        )

    def landed(self, ref, slot):
        self.copy(ref, ref, slot, self.place.partner()).wait_recv()

    def sent(self, ref, slot):
        self.copy(ref, ref, slot, self.place.partner()).wait_send()

    def held_here(self, src, dst):
        self.used_local += 1
        assert self.used_local <= self.local.shape[0]
        return pltpu.make_async_copy(src, dst, self.local.at[self.used_local - 1])

    def here(self, src, dst):
        made = self.held_here(src, dst)
        made.start()
        return made


class Spread:
    def __init__(self, w, parts, homes):
        self.w, self.parts, self.homes = w, parts, homes
        self.slots = [[w.slot() for _ in range(3)] for _ in parts]
        self.first = w.used_local
        w.used_local += len(parts)

    def _kept(self, act):
        t = self.w.place.t
        for n, (part, home) in enumerate(zip(self.parts, self.homes)):
            act(pltpu.make_async_copy(part(t), home(t), self.w.local.at[self.first + n]))

    def start(self):
        p = self.w.place
        for part, home, slots in zip(self.parts, self.homes, self.slots):
            for peer, slot in zip(p.peers, slots):
                self.w.copy(part(peer), home(p.t), slot, p.plane(peer)).start()
        self._kept(lambda made: made.start())

    def wait(self):
        p = self.w.place
        self._kept(lambda made: made.wait())
        for home, slots in zip(self.homes, self.slots):
            for peer, slot in zip(p.peers, slots):
                self.w.landed(home(peer), slot)

    def drain(self):
        p = self.w.place
        for part, slots in zip(self.parts, self.slots):
            for peer, slot in zip(p.peers, slots):
                self.w.sent(part(peer), slot)


class OneSpread:
    def __init__(self, w, part, home):
        self.w, self.part, self.home = w, part, home
        self.slots = [w.slot() for _ in range(3)]
        self.kept = w.held_here(part, home(w.place.t))

    def start(self):
        p = self.w.place

        @pl.when(p.t == p.z)
        def _():
            self.kept.start()

        for peer, slot in zip(p.peers, self.slots):

            @pl.when(peer == p.z)
            def _():
                self.w.copy(self.part, self.home(p.t), slot, p.plane(peer)).start()

    def wait(self):
        p = self.w.place

        @pl.when(p.t == p.z)
        def _():
            self.kept.wait()
            for peer, slot in zip(p.peers, self.slots):
                self.w.landed(self.home(peer), slot)

    def drain(self):
        p = self.w.place
        for peer, slot in zip(p.peers, self.slots):

            @pl.when(peer == p.z)
            def _():
                self.w.sent(self.part, slot)


class LineGather:
    def __init__(self, w, regions):
        self.w, self.regions = w, regions
        self.slots = [
            {key: w.slot() for key in ["o", "r1", "r2", "r3", "l1", "l2", "l3"]
             + ["or1", "or2", "or3", "ol1", "ol2", "ol3"]}
            for _ in regions
        ]

    def _each(self, b, act, *conditions):
        p = self.w.place
        for (view, odd), slots in zip(self.regions, self.slots):
            terms = list(conditions) + ([b == p.t] if odd else [])
            if not terms:
                act(view, slots)
                continue
            ok = terms[0]
            for term in terms[1:]:
                ok = jnp.logical_and(ok, term)

            @pl.when(ok)
            def _():
                act(view, slots)

    def _start(self, view, b, slot, device):
        p = self.w.place
        self.w.copy(view(b, p.c), view(b, p.c), slot, device).start()

    def first(self):
        p = self.w.place
        z = p.z
        self._each(z, lambda v, s: self._start(v, z, s["r1"], p.line(z + 1)), z < 3)
        self._each(z, lambda v, s: self._start(v, z, s["l1"], p.line(z - 1)), z > 0)
        self._each(z, lambda v, s: self._start(v, z, s["o"], p.partner()))

    def step(self, k):
        p = self.w.place
        z = p.z
        for sign, left in ((1, "r"), (-1, "l")):
            b = z - sign * (k - 1)
            exists = b >= 0 if sign > 0 else b <= 3

            def take(v, s):
                self.w.landed(v(b, p.c), s[f"{left}{k - 1}"])
                self._start(v, b, s[f"o{left}{k - 1}"], p.partner())

            self._each(b, take, exists)
            if k < 4:
                more = z < 3 if sign > 0 else z > 0
                self._each(
                    b, lambda v, s: self._start(v, b, s[f"{left}{k}"], p.line(z + sign)), exists, more
                )

    def finish(self):
        p = self.w.place
        z = p.z
        other = 1 - p.c
        self._each(z, lambda v, s: self.w.landed(v(z, other), s["o"]))
        for k in (1, 2, 3):
            for sign, left in ((1, "r"), (-1, "l")):
                b = z - sign * k
                exists = b >= 0 if sign > 0 else b <= 3
                self._each(b, lambda v, s: self.w.landed(v(b, other), s[f"o{left}{k}"]), exists)

    def drain(self):
        p = self.w.place
        z = p.z
        self._each(z, lambda v, s: self.w.sent(v(z, p.c), s["o"]))
        for k in (1, 2, 3):
            for sign, left in ((1, "r"), (-1, "l")):
                b = z - sign * k
                exists = b >= 0 if sign > 0 else b <= 3
                self._each(b, lambda v, s: self.w.sent(v(b, p.c), s[f"o{left}{k}"]), exists)
                b2 = z - sign * (k - 1)
                exists2 = b2 >= 0 if sign > 0 else b2 <= 3
                more = z < 3 if sign > 0 else z > 0
                self._each(b2, lambda v, s: self.w.sent(v(b2, p.c), s[f"{left}{k}"]), exists2, more)


class PlaneGather:
    def __init__(self, w, buf):
        self.w, self.buf = w, buf
        self.half = buf.shape[1] // 2
        self.s = {key: w.slot() for key in ("x", "y", "fx", "fy")}

    def _low(self, t):
        return self.buf.at[t, pl.ds(0, self.half)]

    def _high(self, t):
        return self.buf.at[t, pl.ds(self.half, self.half)]

    def start(self, own=None):
        p, w = self.w.place, self.w
        self.own = self.buf.at[p.t] if own is None else own
        w.copy(self.own, self.buf.at[p.t], self.s["x"], p.plane(p.tx)).start()
        w.copy(self.own, self.buf.at[p.t], self.s["y"], p.plane(p.ty)).start()

    def forward(self):
        p, w = self.w.place, self.w
        w.landed(self.buf.at[p.tx], self.s["x"])
        w.copy(self._high(p.tx), self._high(p.tx), self.s["fy"], p.plane(p.ty)).start()
        w.landed(self.buf.at[p.ty], self.s["y"])
        w.copy(self._low(p.ty), self._low(p.ty), self.s["fx"], p.plane(p.tx)).start()

    def finish(self):
        p, w = self.w.place, self.w
        w.landed(self._low(p.td), self.s["fx"])
        w.landed(self._high(p.td), self.s["fy"])

    def drain(self):
        p, w = self.w.place, self.w
        w.sent(self.own, self.s["x"])
        w.sent(self.own, self.s["y"])
        w.sent(self._high(p.tx), self.s["fy"])
        w.sent(self._low(p.ty), self.s["fx"])


class PlaneSum:
    def __init__(self, w, part, far, near):
        self.w, self.part, self.far, self.near = w, part, far, near
        self.half = part.shape[1] // 2
        self.s = {key: w.slot() for key in ("dx", "dy", "x", "y")}

    def diagonal(self):
        p, w, h = self.w.place, self.w, self.half
        self.a = self.part.at[p.td, pl.ds(0, h)]
        self.b = self.part.at[p.td, pl.ds(h, h)]
        w.copy(self.a, self.far.at[0], self.s["dx"], p.plane(p.tx)).start()
        w.copy(self.b, self.far.at[1], self.s["dy"], p.plane(p.ty)).start()

    def _add(self, t, which):
        h = self.half

        @pl.loop(0, h // 32)
        def _(i):
            rows = pl.ds(pl.multiple_of(i * 32, 32), 32)
            mine = pl.ds(pl.multiple_of(which * h + i * 32, 32), 32)
            total = self.part[t, mine, :].astype(f32) + self.far[which, rows, :].astype(f32)
            self.part[t, mine, :] = total.astype(bf16)

    def arrive(self):
        p = self.w.place
        self.w.landed(self.far.at[0], self.s["dx"])
        self._add(p.ty, 0)
        self.w.landed(self.far.at[1], self.s["dy"])
        self._add(p.tx, 1)

    def to_y(self):
        p, w = self.w.place, self.w
        w.copy(self.part.at[p.ty], self.near.at[1], self.s["y"], p.plane(p.ty)).start()

    def to_x(self):
        p, w = self.w.place, self.w
        w.copy(self.part.at[p.tx], self.near.at[0], self.s["x"], p.plane(p.tx)).start()

    def finish(self):
        self.w.landed(self.near.at[0], self.s["x"])
        self.w.landed(self.near.at[1], self.s["y"])

    def drain(self):
        p, w = self.w.place, self.w
        w.sent(self.a, self.s["dx"])
        w.sent(self.b, self.s["dy"])
        w.sent(self.part.at[p.ty], self.s["y"])
        w.sent(self.part.at[p.tx], self.s["x"])


def add_into(dst, *sources):
    lead, rows = dst.shape[:-2], dst.shape[-2]
    size = 64 if rows % 64 == 0 else rows
    count = rows // size
    total = count
    for n in lead:
        total *= n

    @pl.loop(0, total)
    def _(i):
        at = []
        rest = lax.div(i, count)
        for n in reversed(lead):
            at.insert(0, lax.rem(rest, n))
            rest = lax.div(rest, n)
        at.append(pl.ds(pl.multiple_of(lax.rem(i, count) * size, size), size))
        at = tuple(at)
        value = dst.at[at][...].astype(f32)
        for src in sources:
            value = value + src.at[at][...].astype(f32)
        dst.at[at][...] = value.astype(bf16)


class CoreSum:
    def __init__(self, w, half, landing):
        self.w, self.half, self.landing = w, half, landing
        self.slot = w.slot()

    def start(self):
        p = self.w.place
        self.w.copy(self.half(1 - p.c), self.landing, self.slot, p.partner()).start()

    def finish(self):
        self.w.landed(self.landing, self.slot)
        add_into(self.half(self.w.place.c), self.landing)

    def drain(self):
        self.w.sent(self.half(1 - self.w.place.c), self.slot)


class LineSum:
    def __init__(self, w, parts, odd=None):
        self.w, self.parts, self.odd = w, parts, odd
        self.slots = [[w.slot() for _ in range(6)] for _ in parts]
        if odd is not None:
            self.odd_slots = w.block(3)

    def _each(self, act, ok):
        @pl.when(ok)
        def _():
            for (piece, landing), slots in zip(self.parts, self.slots):
                act(piece, landing, slots)

    def _send(self, k, act, which):
        z = self.w.place.z
        for side, sign in ((0, 1), (1, -1)):
            j = z + sign * (4 - k)
            end = z == 0 if sign > 0 else z == 3
            inner = jnp.logical_and(z > 0, z < 3)
            there = j <= 3 if sign > 0 else j >= 0
            valid = end if which == "end" else jnp.logical_and(inner, there)
            self._each(lambda piece, landing, s: act(piece, landing, s[side * 3 + k - 1], side, k, j, sign), valid)

    def _out(self, piece, landing, slot, side, k, j, sign):
        p = self.w.place
        self.w.copy(piece(j), landing(side, k), slot, p.line(p.z + sign)).start()

    def first(self):
        p = self.w.place
        for k in (1, 2, 3):
            self._send(k, self._out, "end")
        if self.odd is not None:
            piece, landing = self.odd

            @pl.when(p.z != p.t)
            def _():
                k = lax.rem(p.t - p.z + 4, 4) - 1
                self.w.copy(piece, landing(k), self.odd_slots + k, p.line(p.t)).start()

    def _take(self, k):
        z = self.w.place.z
        for side, sign in ((0, 1), (1, -1)):
            j = z - sign + sign * (4 - k)
            valid = jnp.logical_and(j <= 3, z >= 1) if sign > 0 else jnp.logical_and(j >= 0, z <= 2)

            def act(piece, landing, s):
                self.w.landed(landing(side, k), s[side * 3 + k - 1])
                add_into(piece(j), landing(side, k))

            self._each(act, valid)

    def step(self, k):
        self._take(k - 1)
        if k < 4:
            self._send(k, self._out, "inner")
        elif self.odd is not None:
            p = self.w.place
            piece, landing = self.odd

            @pl.when(p.z == p.t)
            def _():
                for n in range(3):
                    self.w.landed(landing(n), self.odd_slots + n)
                add_into(piece, landing(0), landing(1), landing(2))

    def drain(self):
        p = self.w.place
        for k in (1, 2, 3):
            for which in ("end", "inner"):
                self._send(k, lambda piece, landing, slot, side, kk, j, sign: self.w.sent(piece(j), slot), which)
        if self.odd is not None:

            @pl.when(p.z != p.t)
            def _():
                self.w.sent(self.odd[0], self.odd_slots + lax.rem(p.t - p.z + 4, 4) - 1)


class SmallSum:
    def __init__(self, w, places, keep):
        self.w, self.places, self.keep = w, places, keep
        self.slots = [w.block(7) for _ in places]

    def line(self):
        p, w = self.w.place, self.w
        for (own, line, core, plane), s in zip(self.places, self.slots):
            line[p.z] = own[...]
            for k in (1, 2, 3):
                w.copy(own, line.at[p.z], s + k - 1, p.line(p.around(k))).start()

    def core(self):
        p, w = self.w.place, self.w
        for (own, line, core, plane), s in zip(self.places, self.slots):
            for k in (1, 2, 3):
                w.landed(line.at[p.around(4 - k)], s + k - 1)
            core[0] = line[0] + line[1] + line[2] + line[3]
            w.copy(core.at[0], core.at[1], s + 3, p.partner()).start()

    def plane(self):
        p, w = self.w.place, self.w
        for (own, line, core, plane), s in zip(self.places, self.slots):
            w.landed(core.at[1], s + 3)
            core[2] = core[0] + core[1]
            plane[p.t] = core[2]
            for n, peer in enumerate(p.peers):
                w.copy(core.at[2], plane.at[p.t], s + 4 + n, p.plane(peer)).start()

    def result(self):
        p, w = self.w.place, self.w
        values = []
        for (own, line, core, plane), s, keep in zip(self.places, self.slots, self.keep):
            for n, peer in enumerate(p.peers):
                w.landed(plane.at[peer], s + 4 + n)
            values.append(plane[...] if keep else plane[0] + plane[1] + plane[2] + plane[3])
        return values

    def drain(self):
        w = self.w
        for (own, line, core, plane), s in zip(self.places, self.slots):
            for k in (1, 2, 3):
                w.sent(own, s + k - 1)
                w.sent(core.at[2], s + 3 + k)
            w.sent(core.at[0], s + 3)


def stack_rows(v, out):
    for n in range(12):
        out[n : n + 1, :] = v[:, n * 128 : (n + 1) * 128]


class OddScatter:
    def __init__(self, w, part, home):
        self.w, self.part, self.home = w, part, home
        self.slots = [w.slot() for _ in range(3)]
        self.kept = w.held_here(part(w.place.t), home)

    def start(self):
        p = self.w.place

        @pl.when(p.t == p.z)
        def _():
            self.kept.start()
            for peer, slot in zip(p.peers, self.slots):
                self.w.copy(self.part(peer), self.home, slot, p.plane(peer)).start()

    def finish(self):
        p = self.w.place
        for peer, slot in zip(p.peers, self.slots):

            @pl.when(peer == p.z)
            def _():
                self.w.landed(self.home, slot)

        @pl.when(p.t == p.z)
        def _():
            self.kept.wait()
            for peer, slot in zip(p.peers, self.slots):
                self.w.sent(self.part(peer), slot)


def rows16(i, size=16):
    return pl.ds(pl.multiple_of(i * 16, 16), size)


def cols(b, width=128):
    return pl.ds(pl.multiple_of(b * width, width), width)


def norm_rows(v):
    return lax.rsqrt(jnp.mean(v * v, axis=1, keepdims=True) + epsilon)


def log1p_series(y):
    s = y / (2.0 + y)
    q = s * s
    total = 1.0 / 17
    for n in (15, 13, 11, 9, 7, 5, 3, 1):
        total = total * q + 1.0 / n
    return 2.0 * s * total


def turn(src, dst, j):
    @pl.loop(0, 12)
    def _(i):
        dst[cols(i), cols(j, 256)] = src[j, :, cols(i)].T


def fold(state, product):
    rows = [v[0:1, b * 128 : (b + 1) * 128] for v in (state, product) for b in range(4)]
    return jnp.concatenate(rows, axis=0)


def unfold(tile, first):
    return jnp.concatenate([jnp.broadcast_to(tile[first + b : first + b + 1, :], (8, 128)) for b in range(4)], axis=1)


def recurrence_forward(
    x_ref, gain_1d, conv_w, conv_b, gate_bias, decay, wx, wy, wo, gates, wg, wu, wd, cot,
    x1_ref, stat_ref, sm_out,
    n1t_out, win_out, wout_out, wg_out, wu_out, a2d, cot_out, gg_out,
    xb_out, zy_out, zx_out, za_out, c_out, a_out, h_out, o_out,
    win, wout, gg, n1, n1t, xb, zy, zx, za, cc, aa, hh, ac, oo, part, far, near,
    tail, sums, sm_ref, small_ref, gain_ref, send, recv, local,
):
    p = Place()
    w = Wires(p, send, recv, local)
    t, c, z = p.t, p.c, p.z
    odd = pl.ds(1024, 128)
    small_ref[...] = jnp.zeros((16, 512), f32)
    small_ref[0:4, :] = conv_w[...]
    small_ref[4:5, :] = conv_b[...].reshape(1, 512)
    small_ref[5:7, :] = gate_bias[...]
    raw = decay[...].reshape(1, 512)
    small_ref[7:8, :] = jnp.maximum(raw, 0.0) + log1p_series(jnp.exp(-jnp.abs(raw)))
    small_ref[8:9, :] = jax.nn.sigmoid(raw)
    gain_ref[...] = gain_1d[...].reshape(1, 1536)
    p.enter()

    spread_in = Spread(
        w,
        [lambda q: wx.at[:, cols(q)], lambda q: wy.at[:, cols(q)], lambda q: gates.at[:, q]],
        [
            lambda q: win.at[0, q, c, :, cols(z)],
            lambda q: win.at[1, q, c, :, cols(z)],
            lambda q: gg.at[:, z, q, c],
        ],
    )
    spread_out = Spread(w, [lambda q: wo.at[:, cols(q)]], [lambda q: wout.at[q, c, :, cols(z)]])

    def wide(weight, home, odd_home):
        return (
            Spread(w, [lambda q: weight.at[:, cols(q, 256)]], [home]),
            OneSpread(w, weight.at[:, odd], odd_home),
        )

    spreads = [
        wide(wg, lambda q: wg_out.at[q, c, :, cols(z, 256)], lambda q: wg_out.at[q, c, :, odd]),
        wide(wu, lambda q: wu_out.at[q, c, :, cols(z, 256)], lambda q: wu_out.at[q, c, :, odd]),
        wide(wd, lambda q: a2d.at[q, :, pl.ds(0, 256)], lambda q: a2d.at[q, :, pl.ds(256, 128)]),
    ]

    def wide_line(full):
        return LineGather(
            w, [(lambda b, q: full.at[:, q, :, cols(b, 256)], False), (lambda b, q: full.at[:, q, :, odd], True)]
        )

    line_in = LineGather(
        w, [(lambda b, q: win.at[:, :, q, :, cols(b)], False), (lambda b, q: gg.at[:, b, :, q], False)]
    )
    line_out = LineGather(w, [(lambda b, q: wout.at[:, q, :, cols(b)], False)])
    line_g, line_u = wide_line(wg_out), wide_line(wu_out)

    spread_in.start()
    small_slots = [w.slot() for _ in range(3)]
    for k in (1, 2, 3):
        w.copy(
            small_ref.at[:, cols(t)], sm_ref.at[:, cols(z)], small_slots[k - 1], p.line(p.around(k))
        ).start()
    sm_ref[:, cols(z)] = small_ref[:, cols(t)]

    @pl.loop(0, 16)
    def _(i):
        v = x_ref[rows16(i), :].astype(f32)
        n1[t, rows16(i), :] = (v * norm_rows(v) * gain_ref[...]).astype(bf16)

    gather = PlaneGather(w, n1)
    gather.start()
    spread_in.wait()
    line_in.first()
    turn(n1, n1t, t)
    line_in.step(2)
    gather.forward()
    spread_out.start()
    for part_spread in spreads[0] + spreads[1]:
        part_spread.start()
    turn(n1, n1t, p.tx)
    turn(n1, n1t, p.ty)
    line_in.step(3)
    spread_out.wait()
    line_out.first()
    line_in.step(4)
    line_in.finish()
    kept = [w.here(win, win_out), w.here(gg, gg_out)]
    gather.finish()
    gather_cot = PlaneGather(w, cot_out)
    gather_cot.start(cot)

    @pl.loop(0, 4)
    def _(j):
        xb[j, pl.ds(8, 256), :] = mm(n1[j], win[0].reshape(1536, 512))

    halo = w.slot()

    @pl.when(z < 3)
    def _():
        w.copy(xb.at[:, pl.ds(256, 8)], xb.at[:, pl.ds(0, 8)], halo, p.line(z + 1)).start()

    @pl.when(z == 0)
    def _():
        xb[:, 0:8, :] = jnp.zeros((4, 8, 512), f32)

    line_out.step(2)
    turn(n1, n1t, p.td)
    kept.append(w.here(n1t, n1t_out))
    for part_spread in spreads[0]:
        part_spread.wait()
    line_g.first()
    for k in (1, 2, 3):
        w.landed(sm_ref.at[:, cols(p.around(4 - k))], small_slots[k - 1])

    @pl.loop(0, 4)
    def _(j):
        zy[j] = mm(n1[j], win[1].reshape(1536, 512))

    line_out.step(3)
    kept.append(w.here(zy, zy_out))

    @pl.when(z > 0)
    def _():
        w.landed(xb.at[:, pl.ds(0, 8)], halo)

    row = lax.broadcasted_iota(jnp.int32, (8, 512), 0)
    zero = jnp.zeros((8, 512), f32)

    def convolve(j):
        @pl.loop(0, 16)
        def _(i):
            v = xb[j, rows16(i, 24), :]
            total = sm_ref[4:5, :] + sm_ref[0:1, :] * v[8:24]
            for k in (1, 2, 3):
                total = total + sm_ref[k : k + 1, :] * v[8 - k : 24 - k]
            cc[j, rows16(i), :] = total.astype(bf16)

        for b in range(4):
            lanes = pl.ds(b * 128, 128)
            left = cc[j, :, lanes]
            zx[j, :, lanes] = mm(left, gg[0, b].reshape(128, 128)) + sm_ref[5:6, lanes]
            za[j, :, lanes] = mm(left, gg[1, b].reshape(128, 128)) + sm_ref[6:7, lanes]

    def scan(j):
        def advance(i, carry):
            state, product = carry
            pre_x, pre_a = zx[j, rows16(i), :], za[j, rows16(i), :]
            rate, entry = jax.nn.sigmoid(pre_a), jax.nn.sigmoid(pre_x)
            zx[j, rows16(i), :] = entry
            za[j, rows16(i), :] = rate
            log_a = -8.0 * rate * sm_ref[7:8, :]
            decay = jnp.exp(log_a)
            mult = jnp.sqrt(one_minus_square(2.0 * log_a, decay))
            index = lax.broadcasted_iota(jnp.int32, (16, 512), 0) + i * 16 + z * 256
            mult = jnp.where(index == 0, 1.0, mult)
            inflow = mult * entry * cc[j, rows16(i), :].astype(f32)
            aa[j, rows16(i), :] = decay
            for half in (0, 8):
                dv, uv = decay[half : half + 8], inflow[half : half + 8]
                for st in (1, 2, 4):
                    ok = row >= st
                    uv = uv + jnp.where(ok, dv * pltpu.roll(uv, st, 0), 0.0)
                    dv = jnp.where(ok, dv * pltpu.roll(dv, st, 0), dv)
                hv, pv = uv + dv * state, dv * product
                hh[j, pl.ds(pl.multiple_of(i * 16 + half + 8, 8), 8), :] = hv
                ac[j, pl.ds(pl.multiple_of(i * 16 + half, 8), 8), :] = pv
                state = jnp.broadcast_to(hv[7:8, :], (8, 512))
                product = jnp.broadcast_to(pv[7:8, :], (8, 512))
            return state, product

        state, product = lax.fori_loop(0, 16, advance, (zero, zero + 1.0))
        tail[j] = fold(state, product)

    tail_slots = w.block(12)

    def tell(n, j):
        for away in (1, 2, 3):

            @pl.when(z + away <= 3)
            def _():
                w.copy(tail.at[j], sums.at[z, j], tail_slots + 3 * n + away - 1, p.line(z + away)).start()

    def settle(n, j):
        for away in (1, 2, 3):

            @pl.when(z >= away)
            def _():
                w.landed(sums.at[z - away, j], tail_slots + 3 * n + away - 1)

        enter = zero
        for src in range(3):
            tile = sums[src, j]
            enter = jnp.where(z > src, unfold(tile, 0) + unfold(tile, 4) * enter, enter)
        hh[j, 0:8, :] = enter
        first = jnp.concatenate([enter, enter], axis=0)

        @pl.loop(0, 16)
        def _(i):
            at = pl.ds(pl.multiple_of(i * 16 + 8, 8), 16)
            hv = hh[j, at, :] + ac[j, rows16(i), :] * first
            hh[j, at, :] = hv
            oo[j, rows16(i), :] = (hv * gelu_value(zy[j, rows16(i), :])).astype(bf16)

    def project(j):
        for n in range(2):
            part[j, :, n * 768 : (n + 1) * 768] = mm_nt(
                oo[j], wout[2 * n : 2 * n + 2].reshape(768, 512)
            ).astype(bf16)

    summed = PlaneSum(w, part, far, near)
    kept_out = w.held_here(wout, wout_out)

    @pl.loop(0, 5)
    def _(k):
        @pl.when(k < 4)
        def _():
            j = p.member(3 - k)
            convolve(j)
            scan(j)
            tell(k, j)

        @pl.when(k == 0)
        def _():
            line_out.step(4)
            line_g.step(2)
            for part_spread in spreads[1]:
                part_spread.wait()
            line_u.first()

        @pl.when(k == 1)
        def _():
            line_out.finish()
            kept_out.start()

        @pl.when(k == 2)
        def _():
            line_g.step(3)
            line_u.step(2)

        @pl.when(k == 3)
        def _():
            gather_cot.forward()

        @pl.when(k > 0)
        def _():
            j = p.member(4 - k)
            settle(k - 1, j)
            project(j)

        @pl.when(k == 1)
        def _():
            summed.diagonal()

        @pl.when(k == 3)
        def _():
            summed.arrive()
            summed.to_y()
            summed.to_x()

    for part_spread in spreads[2]:
        part_spread.start()
    kept += [w.here(xb, xb_out), w.here(cc, c_out), w.here(zx, zx_out), w.here(za, za_out)]
    kept += [kept_out, w.here(hh, h_out), w.here(oo, o_out)]
    next_slot = w.slot()

    @pl.when(z > 0)
    def _():
        w.copy(aa.at[:, pl.ds(0, 8)], aa.at[:, pl.ds(256, 8)], next_slot, p.line(z - 1)).start()

    @pl.when(z == 3)
    def _():
        aa[:, 256:264, :] = jnp.zeros((4, 8, 512), f32)

    line_g.step(4)
    line_u.step(3)

    @pl.when(z < 3)
    def _():
        w.landed(aa.at[:, pl.ds(256, 8)], next_slot)

    kept.append(w.here(aa, a_out))
    line_g.finish()
    gather_cot.finish()
    summed.finish()

    def last(i, carry):
        at = rows16(i)
        branch = part[t, at, :].astype(f32) + near[0, at, :].astype(f32) + near[1, at, :].astype(f32)
        stream = x_ref[at, :].astype(f32) + branch
        x1_ref[at, :] = stream
        s2, b2 = stream * stream, branch * branch
        return carry[0] + s2[0:8] + s2[8:16], carry[1] + b2[0:8] + b2[8:16]

    zw = jnp.zeros((8, 1536), f32)
    s2, b2 = lax.fori_loop(0, 16, last, (zw, zw))
    stat_ref[...] = zw
    stat_ref[0:1, :] = jnp.sum(s2, axis=0, keepdims=True)
    stat_ref[1:2, :] = jnp.sum(b2, axis=0, keepdims=True)
    sm_out[...] = sm_ref[...]
    line_u.step(4)
    line_u.finish()
    for part_spread in spreads[2]:
        part_spread.wait()
    for made in kept:
        made.wait()
    spread_in.drain()
    spread_out.drain()
    for pair in spreads:
        for part_spread in pair:
            part_spread.drain()
    for k in (1, 2, 3):
        w.sent(small_ref.at[:, cols(t)], small_slots[k - 1])
    gather.drain()
    gather_cot.drain()
    line_in.drain()
    line_out.drain()
    line_g.drain()
    line_u.drain()

    @pl.when(z < 3)
    def _():
        w.sent(xb.at[:, pl.ds(256, 8)], halo)

    for n in range(4):
        for away in (1, 2, 3):

            @pl.when(z + away <= 3)
            def _():
                w.sent(tail.at[n], tail_slots + 3 * n + away - 1)

    @pl.when(z > 0)
    def _():
        w.sent(aa.at[:, pl.ds(0, 8)], next_slot)

    summed.drain()


def shape(dims, dtype):
    return jax.ShapeDtypeStruct(dims, dtype)


def call(kernel, number, args, spaces, outs, out_spaces, scratch, wires, locals_, name):
    v = pl.BlockSpec(memory_space=pltpu.VMEM)
    a = pl.BlockSpec(memory_space=pl.ANY)
    kinds = {"v": v, "a": a}
    return pl.pallas_call(
        kernel,
        out_shape=outs,
        in_specs=[kinds[k] for k in spaces],
        out_specs=[kinds[k] for k in out_spaces],
        scratch_shapes=list(scratch)
        + [
            pltpu.SemaphoreType.DMA((wires,)),
            pltpu.SemaphoreType.DMA((wires,)),
            pltpu.SemaphoreType.DMA((locals_,)),
        ],
        compiler_params=pltpu.CompilerParams(
            collective_id=number, has_side_effects=True, vmem_limit_bytes=VMEM_BYTES
        ),
        name=name,
    )(*args)


def forward_recurrence(*args):
    V = pltpu.VMEM
    outs = [
        shape((256, 1536), f32), shape((8, 1536), f32), shape((16, 512), f32),
        shape((1536, 1024), bf16), shape((2, 4, 2, 192, 512), bf16), shape((4, 2, 192, 512), bf16),
        shape((4, 2, 192, 1152), bf16), shape((4, 2, 192, 1152), bf16), shape((4, 192, 384), bf16),
        shape((4, 256, 1536), bf16), shape((2, 4, 4, 2, 16, 128), bf16),
        shape((4, 264, 512), f32), shape((4, 256, 512), f32), shape((4, 256, 512), f32),
        shape((4, 256, 512), f32), shape((4, 256, 512), bf16), shape((4, 264, 512), f32),
        shape((4, 264, 512), f32), shape((4, 256, 512), bf16),
    ]
    scratch = [
        V((2, 4, 2, 192, 512), bf16), V((4, 2, 192, 512), bf16), V((2, 4, 4, 2, 16, 128), bf16),
        V((4, 256, 1536), bf16), V((1536, 1024), bf16), V((4, 264, 512), f32), V((4, 256, 512), f32),
        V((4, 256, 512), f32), V((4, 256, 512), f32), V((4, 256, 512), bf16),
        V((4, 264, 512), f32), V((4, 264, 512), f32), V((4, 256, 512), f32),
        V((4, 256, 512), bf16), V((4, 256, 1536), bf16), V((2, 128, 1536), bf16),
        V((2, 256, 1536), bf16),
        V((4, 8, 128), f32), V((4, 4, 8, 128), f32), V((16, 512), f32), V((16, 512), f32), V((1, 1536), f32),
    ]
    return call(
        recurrence_forward, 0, args, "v" * 6 + "a" * 8,
        outs, "vvv" + "a" * 16, scratch, 160, 32, "recurrence_forward",
    )


def half_line(w, piece, landing, odd_piece=None, odd_landing=None):
    odd = None if odd_piece is None else (odd_piece, lambda n: odd_landing.at[n])
    return LineSum(w, [(piece, lambda s, k: landing.at[s * 3 + k - 1])], odd)


def feed_forward(
    x1_ref, gain_1d, cot_ref, cot_in, wg_in, wu_in, a2d,
    dx1_ref, y_ref, stat_ref, half_out, piece_out,
    wgu, wd, n2, n2t, ct, ctt, gu, hid, dgu, part, far, near,
    gdown, cb, landing, landing_odd, gain_ref, send, recv, local,
):
    p = Place()
    w = Wires(p, send, recv, local)
    t, c, z = p.t, p.c, p.z
    gain_ref[...] = gain_1d[...].reshape(1, 1536)
    p.enter()
    odd = pl.ds(1024, 128)

    first = w.here(a2d.at[:, :, pl.ds(0, 256)], wd.at[:, c, :, cols(z, 256)])
    first_odd = w.held_here(a2d.at[:, :, pl.ds(256, 128)], wd.at[:, c, :, odd])

    @pl.when(t == z)
    def _():
        first_odd.start()

    load_gate, load_up = w.here(wg_in, wgu.at[0]), w.here(wu_in, wgu.at[1])
    load_cot = [w.here(cot_in.at[j], ct.at[j]) for j in p.peers]

    @pl.loop(0, 16)
    def _(i):
        at = rows16(i)
        v = x1_ref[at, :]
        n2[t, at, :] = (v * norm_rows(v) * gain_ref[...]).astype(bf16)
        ct[t, at, :] = cot_ref[at, :]

    gather = PlaneGather(w, n2)
    gather.start()
    first.wait()

    @pl.when(t == z)
    def _():
        first_odd.wait()

    line_d = LineGather(
        w, [(lambda b, q: wd.at[:, q, :, cols(b, 256)], False), (lambda b, q: wd.at[:, q, :, odd], True)]
    )
    line_d.first()
    load_gate.wait()
    load_up.wait()

    @pl.loop(0, 4)
    def _(k):
        @pl.when(k == 1)
        def _():
            for made in load_cot:
                made.wait()

            @pl.loop(0, 4)
            def _(n):
                turn(ct, ctt, n)

            line_d.step(2)
            gather.forward()
            line_d.step(3)

        @pl.when(k == 3)
        def _():
            gather.finish()

        j = p.member(k)

        @pl.loop(0, 2)
        def _(m):
            gu[m, j] = mm(n2[j], wgu[m].reshape(1536, 1152))

        @pl.loop(0, 16)
        def _(i):
            at = rows16(i)
            value, slope = gelu_pair(gu[0, j, at, :])
            u = gu[1, j, at, :]
            hid[j, at, :] = (value * u).astype(bf16)
            gu[0, j, at, :] = u * slope
            gu[1, j, at, :] = value

        @pl.when(k < 3)
        def _():
            turn(n2, n2t, j)

    line_d.step(4)
    line_d.finish()

    def weight_grad(left, right, out, first, count):
        @pl.loop(first, first + count)
        def _(i):
            out[i] = mm(left[cols(i, 384), :], right[...].reshape(1024, 1152)).astype(bf16).reshape(2, 192, 1152)

    def half_unit(home, u, n):
        return half_line(
            w,
            lambda j: home.at[pl.ds(2 * u, 2), c, :, cols(j, 256)],
            landing.at[n],
            home.at[pl.ds(2 * u, 2), c, :, odd],
            landing_odd.at[n],
        )

    units = [half_unit(gdown, 0, 0), half_unit(gdown, 1, 1), half_unit(wgu.at[0], 0, 2)]
    cores = [
        CoreSum(w, lambda q, u=u: gdown.at[pl.ds(2 * u, 2), q], cb.at[0, pl.ds(2 * u, 2)]) for u in range(2)
    ]
    cores_gu = [CoreSum(w, lambda q, m=m: wgu.at[m, :, q], cb.at[1 - m]) for m in range(2)]
    summed = PlaneSum(w, part, far, near)
    near_m = n2.at[pl.ds(0, 2)]
    branch = PlaneSum(w, ct, far, near_m)

    def mid(j):
        for n in range(2):
            ct[j, :, n * 768 : (n + 1) * 768] = mm_nt(
                hid[j], wd[2 * n : 2 * n + 2].reshape(768, 1152)
            ).astype(bf16)

    @pl.loop(0, 4)
    def _(k):
        j = p.member(3 - k)
        dh = mm(ct[j], wd[...].reshape(1536, 1152))
        for m in range(2):
            dgu[m, j] = (dh * gu[m, j]).astype(bf16)

        for n in range(2):
            span = pl.ds(2 * n, 2)
            part[j, :, n * 768 : (n + 1) * 768] = (
                mm_nt(dgu[0, j], wgu[0, span].reshape(768, 1152)) + mm_nt(dgu[1, j], wgu[1, span].reshape(768, 1152))
            ).astype(bf16)

        @pl.when(k == 0)
        def _():
            summed.diagonal()
            turn(n2, n2t, p.td)

        @pl.when(k == 1)
        def _():
            cores[0].finish()
            units[0].first()

        @pl.when(k == 2)
        def _():
            summed.arrive()
            summed.to_y()
            summed.to_x()
            cores[1].finish()
            units[1].first()

        @pl.when(k < 2)
        def _():
            weight_grad(ctt, hid, gdown, 2 * k, 2)

        @pl.when(k == 0)
        def _():
            cores[0].start()

        @pl.when(k == 1)
        def _():
            cores[1].start()

    units[0].step(2)

    @pl.loop(0, 2)
    def _(m):
        weight_grad(n2t, dgu.at[m], wgu.at[m], 0, 4)

        @pl.when(m == 0)
        def _():
            cores_gu[0].start()
            units[0].step(3)

        @pl.when(m == 1)
        def _():
            cores_gu[0].finish()
            cores_gu[1].start()
            units[2].first()

        for i in range(2):
            mid(p.member(3 - 2 * m - i))

    units[0].step(4)
    units[1].step(2)
    summed.finish()
    gather.drain()
    branch.diagonal()

    def dx(i, carry):
        at = rows16(i)
        v = x1_ref[at, :]
        s = norm_rows(v)
        dn = part[t, at, :].astype(f32) + near[0, at, :].astype(f32) + near[1, at, :].astype(f32)
        q = gain_ref[...] * dn
        dx1_ref[at, :] = (
            cot_ref[at, :].astype(f32) + s * q - v * (s * s * s * jnp.mean(q * v, axis=1, keepdims=True))
        )
        g2 = dn * v * s
        return carry + g2[0:8] + g2[8:16]

    zw = jnp.zeros((8, 1536), f32)
    g2 = lax.fori_loop(0, 16, dx, zw)
    stat_ref[...] = zw
    stat_ref[4:5, :] = jnp.sum(g2, axis=0, keepdims=True)
    units[1].step(3)
    cores_gu[1].finish()
    kept = [w.here(wgu.at[1, :, c], half_out.at[1])]
    branch.arrive()
    branch.to_y()
    branch.to_x()
    units[1].step(4)
    for src, dst in ((cols(z, 256), pl.ds(0, 256)), (odd, pl.ds(256, 128))):
        kept.append(w.here(gdown.at[:, c, :, src], piece_out.at[:, :, dst]))
    units[2].step(2)
    units[2].step(3)
    units[2].step(4)
    kept.append(w.here(wgu.at[0, :, c], half_out.at[0]))
    branch.finish()

    def last(i, carry):
        at = rows16(i)
        m = ct[t, at, :].astype(f32) + n2[0, at, :].astype(f32) + n2[1, at, :].astype(f32)
        y = x1_ref[at, :] + m
        y_ref[at, :] = y.astype(bf16)
        m2, y2 = m * m, y * y
        return carry[0] + m2[0:8] + m2[8:16], carry[1] + y2[0:8] + y2[8:16]

    m2, y2 = lax.fori_loop(0, 16, last, (zw, zw))
    stat_ref[2:3, :] = jnp.sum(m2, axis=0, keepdims=True)
    stat_ref[3:4, :] = jnp.sum(y2, axis=0, keepdims=True)
    for made in kept:
        made.wait()
    line_d.drain()
    summed.drain()
    branch.drain()
    for unit in units + cores + cores_gu:
        unit.drain()


def recurrence_backward(
    x_ref, gain_1d, dx1_ref, sm_ref, stat1, stat2,
    win_in, wout_in, n1t_in, xb_in, zy_in, zx_in, za_in, c_in, a_in, h_in, o_in, gg_in,
    half_in, piece_in,
    gi_ref, v1_ref, v2_ref, v3_ref, gin_out, gout_out, gff_out, gd_out, ggate_out,
    win, wout, n1t, dr, xb, zy, zx, za, cc, aa, hh, oo, gg, hgu, tmp, bc, dzy, dzx, dza,
    far, near, gin, gout, ggr, cbi, cbo, cbg, land_i, land_o, land_g, land_f, land_fo,
    tail, sums, acc8, early_own, late_own, acc8_l, acc8_c, acc8_p, early_l, early_c, early_p, late_l, late_c, late_p,
    gain_ref, acc, send, recv, local,
):
    p = Place()
    w = Wires(p, send, recv, local)
    t, c, z = p.t, p.c, p.z
    gain_ref[...] = gain_1d[...].reshape(1, 1536)
    p.enter()
    odd = pl.ds(1024, 128)

    load_half = w.here(half_in, hgu)
    load_out = w.here(wout_in, wout)
    early = [w.here(a, b) for a, b in ((zy_in, zy), (h_in, hh), (a_in, aa))]
    later = [
        w.here(a, b)
        for a, b in (
            (o_in, oo), (zx_in, zx), (za_in, za), (c_in, cc), (gg_in, gg), (n1t_in, n1t), (xb_in, xb), (win_in, win),
        )
    ]

    @pl.loop(0, 16)
    def _(i):
        dr[t, rows16(i), :] = dx1_ref[rows16(i), :].astype(bf16)

    gather = PlaneGather(w, dr)
    gather.start()
    units = [
        half_line(
            w,
            lambda j, m=m, u=u: hgu.at[m, pl.ds(2 * u, 2), :, cols(j, 256)],
            land_f.at[n],
            hgu.at[m, pl.ds(2 * u, 2), :, odd],
            land_fo.at[n],
        )
        for n, (m, u) in enumerate(((0, 1), (1, 0), (1, 1)))
    ]
    line_o = half_line(w, lambda j: gout.at[:, c, :, cols(j)], land_o)
    line_y = half_line(w, lambda j: gin.at[1, :, c, :, cols(j)], land_i.at[1])
    line_x = LineSum(
        w,
        [
            (lambda j: gin.at[0, :, c, :, cols(j)], lambda s, k: land_i.at[0, s * 3 + k - 1]),
            (lambda j: ggr.at[:, j, :, c], lambda s, k: land_g.at[s * 3 + k - 1]),
        ],
    )

    load_half.wait()
    for unit in units:
        unit.first()
    load_out.wait()
    for made in early:
        made.wait()

    row = lax.broadcasted_iota(jnp.int32, (8, 512), 0)
    zero = jnp.zeros((8, 512), f32)

    def scan_rows(j):
        tmp[...] = mm(dr[j], wout[...].reshape(1536, 512))

        def step(k, carry):
            i = 15 - k
            state, product = carry
            at = rows16(i)
            value, slope = gelu_pair(zy[j, at, :])
            do = tmp[at, :]
            h = hh[j, pl.ds(pl.multiple_of(i * 16 + 8, 8), 16), :]
            dzy[j, at, :] = (do * h * slope).astype(bf16)
            flow = do * value
            follow = aa[j, rows16(i, 24), :][1:17]
            for half in (8, 0):
                uv, dv = flow[half : half + 8], follow[half : half + 8]
                for st in (1, 2, 4):
                    ok = row < 8 - st
                    uv = uv + jnp.where(ok, dv * pltpu.roll(uv, 8 - st, 0), 0.0)
                    dv = jnp.where(ok, dv * pltpu.roll(dv, 8 - st, 0), dv)
                gv, pv = uv + dv * state, dv * product
                here = pl.ds(pl.multiple_of(i * 16 + half, 8), 8)
                zy[j, here, :] = gv
                bc[j, here, :] = pv
                state = jnp.broadcast_to(gv[0:1, :], (8, 512))
                product = jnp.broadcast_to(pv[0:1, :], (8, 512))
            return state, product

        state, product = lax.fori_loop(0, 16, step, (zero, zero + 1.0))
        tail[j] = fold(state, product)

    tail_slots = w.block(12)
    down = Spread(
        w, [lambda q: piece_in.at[q, :, pl.ds(0, 256)]], [lambda q: gd_out.at[:, cols(q, 256)]]
    )
    down_odd = OddScatter(w, lambda q: piece_in.at[q, :, pl.ds(256, 128)], gd_out.at[:, odd])

    @pl.loop(0, 4)
    def _(k):
        @pl.when(k == 1)
        def _():
            units[0].step(2)
            gather.forward()
            units[0].step(3)

        @pl.when(k == 3)
        def _():
            gather.finish()
            down.start()
            down_odd.start()
            units[0].step(4)
            units[1].step(2)

        j = p.member(k)
        scan_rows(j)
        for away in (1, 2, 3):

            @pl.when(z >= away)
            def _():
                w.copy(tail.at[j], sums.at[z, j], tail_slots + 3 * k + away - 1, p.line(z - away)).start()

    units[1].step(3)
    for made in later:
        made.wait()

    @pl.loop(0, 4)
    def _(i):
        gout[i] = (
            mm_tn(dr[:, :, cols(i, 384)].reshape(1024, 384), oo[...].reshape(1024, 512))
            .astype(bf16)
            .reshape(2, 192, 512)
        )

    core_o = CoreSum(w, lambda q: gout.at[:, q], cbo)
    core_o.start()

    def in_grad(m, right):
        @pl.loop(0, 4)
        def _(i):
            gin[m, i] = mm(n1t[cols(i, 384), :], right[...].reshape(1024, 512)).astype(bf16).reshape(2, 192, 512)

    in_grad(1, dzy)
    core_y = CoreSum(w, lambda q: gin.at[1, :, q], cbi.at[1])
    core_y.start()
    def through(j, carry):
        after = zero
        for src in (3, 2, 1):
            tile = sums[src, j]
            after = jnp.where(z < src, unfold(tile, 0) + unfold(tile, 4) * after, after)
        after = jnp.concatenate([after, after], axis=0)

        def step(i, carry):
            sum_x, sum_a, sum_d = carry
            at = rows16(i)
            g = zy[j, at, :] + bc[j, at, :] * after
            before = hh[j, rows16(i, 24), :][7:23]
            entry, rate, value = zx[j, at, :], za[j, at, :], cc[j, at, :].astype(f32)
            log_a = -8.0 * rate * sm_ref[7:8, :]
            decay = aa[j, at, :]
            index = lax.broadcasted_iota(jnp.int32, (16, 512), 0) + i * 16 + z * 256
            start = index == 0
            mult = jnp.where(start, 1.0, jnp.sqrt(one_minus_square(2.0 * log_a, decay)))
            gm = g * mult
            d_entry = gm * value
            bc[j, at, :] = gm * entry
            low_x = (d_entry * entry * (1.0 - entry)).astype(bf16)
            dzx[j, at, :] = low_x
            d_mult = g * entry * value
            d_log = g * before * decay - jnp.where(start, 0.0, d_mult * decay * decay / mult)
            low_a = (d_log * (-8.0 * sm_ref[7:8, :]) * rate * (1.0 - rate)).astype(bf16)
            dza[j, at, :] = low_a
            wide_x, wide_a, d_decay = low_x.astype(f32), low_a.astype(f32), d_log * rate
            return (
                sum_x + wide_x[0:8] + wide_x[8:16],
                sum_a + wide_a[0:8] + wide_a[8:16],
                sum_d + d_decay[0:8] + d_decay[8:16],
            )

        carry = lax.fori_loop(0, 16, step, carry)
        for b in range(4):
            lanes = pl.ds(b * 128, 128)
            bc[j, pl.ds(0, 256), lanes] += mm_nt(
                dzx[j, :, lanes], gg[0, b].reshape(128, 128)
            ) + mm_nt(dza[j, :, lanes], gg[1, b].reshape(128, 128))
        return carry

    def taps(j, carry):
        def step(i, carry):
            at = rows16(i)
            v = bc[j, rows16(i, 24), :]
            xv = xb[j, rows16(i, 24), :]
            total = sm_ref[0:1, :] * v[0:16]
            for k in (1, 2, 3):
                total = total + sm_ref[k : k + 1, :] * v[k : k + 16]
            oo[j, at, :] = total.astype(bf16)
            now = v[0:16]
            new = []
            for k in range(4):
                product = now * xv[8 - k : 24 - k]
                new.append(carry[k] + product[0:8] + product[8:16])
            new.append(carry[4] + now[0:8] + now[8:16])
            return tuple(new)

        return lax.fori_loop(0, 16, step, carry)

    halo_slots = w.block(4)

    def tell(n, j):
        @pl.when(z > 0)
        def _():
            w.copy(
                bc.at[j, pl.ds(0, 8)], bc.at[j, pl.ds(256, 8)], halo_slots + n, p.line(z - 1)
            ).start()

    def hear(n, j):
        @pl.when(z < 3)
        def _():
            w.landed(bc.at[j, pl.ds(256, 8)], halo_slots + n)

    @pl.when(z == 3)
    def _():
        bc[:, 256:264, :] = jnp.zeros((4, 8, 512), f32)

    def gate_grads(i, right):
        for b in range(4):
            lanes = pl.ds(b * 128, 128)
            ggr[i, b] = (
                mm_tn(cc[:, :, lanes].reshape(1024, 128), right[:, :, lanes].reshape(1024, 128))
                .astype(bf16)
                .reshape(4, 2, 16, 128)
            )

    gather.drain()
    summed = PlaneSum(w, dr, far, near)
    core_x = CoreSum(w, lambda q: gin.at[0, :, q], cbi.at[0])
    core_g = CoreSum(w, lambda q: ggr.at[:, :, :, q], cbg)
    spreads = [
        Spread(
            w,
            [lambda q: hgu.at[:, q, :, cols(z, 256)]],
            [lambda q: gff_out.at[:, :, cols(q, 256)]],
        ),
        Spread(
            w,
            [lambda q: gout.at[q, c, :, cols(z)], lambda q: gin.at[1, q, c, :, cols(z)]],
            [lambda q: gout_out.at[:, cols(q)], lambda q: gin_out.at[1, :, cols(q)]],
        ),
        Spread(
            w,
            [lambda q: gin.at[0, q, c, :, cols(z)], lambda q: ggr.at[:, z, q, c]],
            [lambda q: gin_out.at[0, :, cols(q)], lambda q: ggate_out.at[:, q]],
        ),
    ]
    odds = [
        OddScatter(w, lambda q: hgu.at[:, q, :, odd], gff_out.at[:, :, odd]),
    ]

    zw = jnp.zeros((8, 1536), f32)
    stats = stat1[...] + stat2[...]
    early_own[...] = jnp.zeros((16, 128), f32)
    stack_rows(stats[4:5, :], early_own)
    for n in range(4):
        early_own[12 + n : 13 + n, :] = jnp.broadcast_to(jnp.sum(stats[n : n + 1, :], axis=1, keepdims=True), (1, 128))
    late_own[...] = jnp.zeros((16, 128), f32)
    small_early = SmallSum(
        w, [(acc8, acc8_l, acc8_c, acc8_p), (early_own, early_l, early_c, early_p)], [True, False]
    )
    small_late = SmallSum(w, [(late_own, late_l, late_c, late_p)], [False])
    acc[...] = jnp.zeros((8, 8, 512), f32)

    @pl.loop(0, 5)
    def _(k):
        @pl.when(k == 1)
        def _():
            units[1].step(4)
            units[2].step(2)

        @pl.when(k == 4)
        def _():
            gate_grads(0, dzx)
            gate_grads(1, dza)

        @pl.when(k < 4)
        def _():
            j = p.member(3 - k)
            for away in (1, 2, 3):

                @pl.when(z + away <= 3)
                def _():
                    w.landed(sums.at[z + away, j], tail_slots + 3 * (3 - k) + away - 1)

            for n, value in enumerate(through(j, (zero,) * 3)):
                acc[n] += value
            tell(k, j)

        @pl.when(k > 0)
        def _():
            j = p.member(4 - k)
            hear(k - 1, j)
            for n, value in enumerate(taps(j, (zero,) * 5)):
                acc[3 + n] += value
            for n in range(2):
                span = pl.ds(2 * n, 2)
                dr[j, :, n * 768 : (n + 1) * 768] = (
                    mm_nt(oo[j], win[0, span].reshape(768, 512)) + mm_nt(dzy[j], win[1, span].reshape(768, 512))
                ).astype(bf16)

        @pl.when(k == 0)
        def _():
            core_o.finish()
            line_o.first()
            core_y.finish()
            line_y.first()

        @pl.when(k == 1)
        def _():
            summed.diagonal()
            units[2].step(3)

        @pl.when(k == 2)
        def _():
            units[2].step(4)
            spreads[0].start()
            odds[0].start()
            line_o.step(2)

        @pl.when(k == 3)
        def _():
            summed.arrive()
            summed.to_y()
            summed.to_x()
            line_o.step(3)

    line_o.step(4)
    in_grad(0, oo)
    core_x.start()
    core_g.start()
    line_y.step(2)
    acc8[5:6, :] = jnp.sum(acc[0], axis=0, keepdims=True)
    acc8[6:7, :] = jnp.sum(acc[1], axis=0, keepdims=True)
    acc8[7:8, :] = -8.0 * sm_ref[8:9, :] * jnp.sum(acc[2], axis=0, keepdims=True)
    for k in range(5):
        acc8[k : k + 1, :] = jnp.sum(acc[3 + k], axis=0, keepdims=True)
    small_early.line()
    core_x.finish()
    core_g.finish()
    line_x.first()
    line_y.step(3)
    line_y.step(4)
    spreads[1].start()
    line_x.step(2)
    small_early.core()
    summed.finish()

    def last(i, carry):
        at = rows16(i)
        v = x_ref[at, :].astype(f32)
        s = norm_rows(v)
        dn = dr[t, at, :].astype(f32) + near[0, at, :].astype(f32) + near[1, at, :].astype(f32)
        q = gain_ref[...] * dn
        gi_ref[at, :] = (
            dx1_ref[at, :] + s * q - v * (s * s * s * jnp.mean(q * v, axis=1, keepdims=True))
        ).astype(bf16)
        g1 = dn * v * s
        return carry + g1[0:8] + g1[8:16]

    g1 = lax.fori_loop(0, 16, last, zw)
    line_x.step(3)
    stack_rows(jnp.sum(g1, axis=0, keepdims=True), late_own)
    small_late.line()
    small_early.plane()
    line_x.step(4)
    spreads[2].start()
    small_late.core()
    small_late.plane()
    v2_ref[...], v1_ref[...] = small_early.result()
    (v3_ref[...],) = small_late.result()

    for made in spreads + [down]:
        made.wait()
        made.drain()
    for made in odds + [down_odd]:
        made.finish()
    small_early.drain()
    small_late.drain()
    summed.drain()
    for made in units + [line_o, line_y, line_x, core_o, core_y, core_x, core_g]:
        made.drain()

    for n in range(4):
        for away in (1, 2, 3):

            @pl.when(z >= away)
            def _():
                w.sent(tail.at[n], tail_slots + 3 * n + away - 1)

    for n in range(4):

        @pl.when(z > 0)
        def _():
            w.sent(bc.at[n, pl.ds(0, 8)], halo_slots + n)


def feed_forward_call(*args):
    V = pltpu.VMEM
    outs = [
        shape((256, 1536), f32), shape((256, 1536), bf16), shape((8, 1536), f32),
        shape((2, 4, 192, 1152), bf16), shape((4, 192, 384), bf16),
    ]
    weights = V((4, 2, 192, 1152), bf16)
    tokens, turned = V((4, 256, 1536), bf16), V((1536, 1024), bf16)
    scratch = [
        V((2, 4, 2, 192, 1152), bf16), weights, tokens, turned, tokens, turned, V((2, 4, 256, 1152), f32),
        V((4, 256, 1152), bf16), V((2, 4, 256, 1152), bf16), tokens, V((2, 128, 1536), bf16),
        V((2, 256, 1536), bf16), weights, V((2, 4, 192, 1152), bf16),
        V((3, 6, 2, 192, 256), bf16), V((3, 3, 2, 192, 128), bf16), V((1, 1536), f32),
    ]
    return call(feed_forward, 1, args, "vvvaaaa", outs, "vvvaa", scratch, 128, 24, "feed_forward")


def backward_recurrence(*args):
    V = pltpu.VMEM
    outs = [
        shape((256, 1536), bf16), shape((16, 128), f32), shape((4, 8, 512), f32), shape((16, 128), f32),
        shape((2, 192, 512), bf16), shape((192, 512), bf16), shape((2, 192, 1152), bf16), shape((192, 1152), bf16),
        shape((2, 4, 16, 128), bf16),
    ]
    tokens, turned = V((4, 256, 1536), bf16), V((1536, 1024), bf16)
    wide, padded, low = V((4, 256, 512), f32), V((4, 264, 512), f32), V((4, 256, 512), bf16)
    scratch = [
        V((2, 4, 2, 192, 512), bf16), V((4, 2, 192, 512), bf16), turned, tokens, padded, wide, wide, wide, low,
        padded, padded, low, V((2, 4, 4, 2, 16, 128), bf16), V((2, 4, 192, 1152), bf16), V((256, 512), f32),
        padded, low, low, low,
        V((2, 128, 1536), bf16), V((2, 256, 1536), bf16),
        V((2, 4, 2, 192, 512), bf16), V((4, 2, 192, 512), bf16), V((2, 4, 4, 2, 16, 128), bf16),
        V((2, 4, 192, 512), bf16), V((4, 192, 512), bf16), V((2, 4, 4, 16, 128), bf16),
        V((2, 6, 4, 192, 128), bf16), V((6, 4, 192, 128), bf16), V((6, 2, 4, 16, 128), bf16),
        V((3, 6, 2, 192, 256), bf16), V((3, 3, 2, 192, 128), bf16),
        V((4, 8, 128), f32), V((4, 4, 8, 128), f32), V((8, 512), f32),
        V((16, 128), f32), V((16, 128), f32), V((4, 8, 512), f32), V((3, 8, 512), f32), V((4, 8, 512), f32),
        V((4, 16, 128), f32), V((3, 16, 128), f32), V((4, 16, 128), f32),
        V((4, 16, 128), f32), V((3, 16, 128), f32), V((4, 16, 128), f32),
        V((1, 1536), f32), V((8, 8, 512), f32),
    ]
    return call(
        recurrence_backward, 2, args, "vvvvvv" + "a" * 14,
        outs, "vvvvaaaaa", scratch, 192, 24, "recurrence_backward",
    )


def finish(count, gin, gout, gff, gd, ggate, y, gi, v1, v2, v3,
           wx, wy, wo, wg, wu, wd, gg, y_out, gi_out, g1, g2, cw, cb, bias, decay, rms, rows, wide):
    wx[...] = gin[0].astype(f32)
    wy[...] = gin[1].astype(f32)
    wo[...] = gout[...].astype(f32)
    wg[...] = gff[0].astype(f32)
    wu[...] = gff[1].astype(f32)
    wd[...] = gd[...].astype(f32)
    y_out[...] = y[...]
    gi_out[...] = gi[...]

    @pl.when(pl.program_id(0) == 0)
    def _():
        gg[...] = ggate[...].astype(f32)
        for n in range(12):
            wide[0:1, n * 128 : (n + 1) * 128] = v3[n : n + 1, :]
            wide[1:2, n * 128 : (n + 1) * 128] = v1[n : n + 1, :]
        g1[...] = wide[0:1, :].reshape(1536)
        g2[...] = wide[1:2, :].reshape(1536)
        for t in range(4):
            for z in range(4):
                rows[:, z * 512 + t * 128 : z * 512 + (t + 1) * 128] = v2[t, :, z * 128 : (z + 1) * 128]
        cw[...] = rows[0:4, :]
        cb[...] = rows[4:5, :].reshape(2048)
        bias[...] = rows[5:7, :]
        decay[...] = rows[7:8, :].reshape(2048)
        root = jnp.sqrt(v1[12:16, :] / count)
        for i in range(4):
            rms[i] = root[i, 0]


def finish_call(count, gin, gout, gff, gd, ggate, y, gi, v1, v2, v3):
    steps = 4

    def sliced(a):
        axis = a.ndim - 2
        block = tuple(n // steps if i == axis else n for i, n in enumerate(a.shape))
        return pl.BlockSpec(block, lambda i: tuple(i if n == axis else 0 for n in range(a.ndim)))

    def whole(a):
        return pl.BlockSpec(a.shape, lambda i: (0,) * len(a.shape))

    one, two = shape((192, 512), f32), shape((192, 1152), f32)
    big = [one, one, one, two, two, two]
    small = [
        shape((1536,), f32), shape((1536,), f32), shape((4, 2048), f32), shape((2048,), f32),
        shape((2, 2048), f32), shape((2048,), f32),
    ]
    gates = shape(ggate.shape, f32)
    tokens = shape(y.shape, bf16)
    return pl.pallas_call(
        functools.partial(finish, count),
        out_shape=big + [gates, tokens, tokens] + small + [shape((4,), f32)],
        grid=(steps,),
        in_specs=[sliced(a) for a in (gin, gout, gff, gd)] + [whole(ggate)] + [sliced(a) for a in (y, gi)] + [whole(v1), whole(v2), whole(v3)],
        out_specs=[sliced(a) for a in big] + [whole(gates), sliced(tokens), sliced(tokens)]
        + [whole(a) for a in small] + [pl.BlockSpec(memory_space=pltpu.SMEM)],
        scratch_shapes=[pltpu.VMEM((8, 2048), f32), pltpu.VMEM((8, 1536), f32)],
        name="finish",
    )(gin, gout, gff, gd, ggate, y, gi, v1, v2, v3)


def fast_local(
    inputs, norm1_gain, w_in_x, w_in_y, conv_w, conv_b, gates, gate_bias, decay_param, w_out,
    norm2_gain, w_gate, w_up, w_down, cotangent,
):
    (x1, stat1, sm, n1t, win, wout, wg, wu, a2d, cot, gg, xb, zy, zx, za, cc, aa, hh, oo) = forward_recurrence(
        inputs, norm1_gain, conv_w, conv_b, gate_bias, decay_param, w_in_x, w_in_y, w_out, gates,
        w_gate, w_up, w_down, cotangent,
    )
    dx1, y, stat2, halves, piece = feed_forward_call(x1, norm2_gain, cotangent, cot, wg, wu, a2d)
    gi, v1, v2, v3, gin, gout, gff, gd, ggate = backward_recurrence(
        inputs, norm1_gain, dx1, sm, stat1, stat2, win, wout, n1t, xb, zy, zx, za, cc, aa, hh, oo, gg,
        halves, piece,
    )
    count = inputs.shape[0] * lax.axis_size("dp") * lax.axis_size("tensor") * inputs.shape[1]
    (gwx, gwy, gwo, gwg, gwu, gwd, ggates, output, grad_inputs, g1, g2, gcw, gcb, gbias, gdecay, rms) = finish_call(
        count, gin, gout, gff, gd, ggate, y, gi, v1, v2, v3
    )
    return (
        output, grad_inputs, g1, gwx, gwy, gcw, gcb, ggates, gbias, gdecay, gwo, g2, gwg, gwu, gwd, rms,
    )


def solution(mesh):
    fits = mesh.shape["dp"] == 8 and mesh.shape["tensor"] == 4
    return jax.shard_map(
        fast_local if fits else local,
        mesh=mesh,
        in_specs=(
            P(("dp", "tensor"), None),
            P(),
            P("dp", "tensor"),
            P("dp", "tensor"),
            P(None, "tensor"),
            P("tensor"),
            P(None, "tensor", "dp", None),
            P(None, "tensor"),
            P("tensor"),
            P("dp", "tensor"),
            P(),
            P("dp", "tensor"),
            P("dp", "tensor"),
            P("dp", "tensor"),
            P(("dp", "tensor"), None),
        ),
        out_specs=(
            P(("dp", "tensor"), None),
            P(("dp", "tensor"), None),
            P(),
            P("dp", "tensor"),
            P("dp", "tensor"),
            P(),
            P(),
            P(None, "tensor", "dp", None),
            P(),
            P(),
            P("dp", "tensor"),
            P(),
            P("dp", "tensor"),
            P("dp", "tensor"),
            P("dp", "tensor"),
            P(),
        ),
        check_vma=False,
    )
```

time: 454 us -> 382 us (0.84); the launches traced: 445 us -> 379 us
  Pallas kernels: 424 us -> 378 us
  local copies, waits for them, and re-layouts: 10.6 us -> 0 us
  other arithmetic: 9.62 us -> 0 us
    pallas_call x3, Pallas kernels: 424 us -> 373 us  [call(): pl.pallas_call(kernel, out_shape=outs, in_specs=[kinds[k] for k in spaces...]
    convert_element_type x5 -> x0, other arithmetic: 7.38 us -> none  [the longest x1 1.99 us: fast_local(): gin[1].astype(f32)]
    pallas_call x0 -> x1, Pallas kernels: none -> 5.21 us  [finish_call(): pl.pallas_call(functools.partial(finish, count), out_shape=big + [gates,...]
where the time goes in v2:
time: 382 us; the launch traced here: 379 us
  Pallas kernels  378 us (99%)
    pallas_call x3, Pallas kernels, call(): pl.pallas_call(kernel, out_shape=outs, in_specs=[kinds[k] for k in spaces...  373 us

profile of v2, /device:TPU:4, one launch (start us, length us, event | category | flops | bytes accessed | tf_op | source)
XLA Modules:
  0.0 378.8 jit_solution(5054762641589532374)
XLA Ops:
  0.7 126.1 %recurrence_forward.1 = (f32[256,1536]{1,0:T(8,128)}, f32[8,1536]{1,0:T(8,128)}, f32[16,512]{1,0:T(8,128)}, bf16[1536,1024]{1,0:T(8,128)(2,1)}, bf16[2,4,2,192,5...) custom-call(bf16[256,1536]{1,0:T(8,128)(2,1)} %x_ref.3, ...), custom_call_target="tpu_custom_call" | custom-call | tf_op jit(solution)/shard_map/recurrence_forward/pallas_call | solution.py:1205
  126.8 118.2 %feed_forward.1 = (f32[256,1536]{1,0:T(8,128)}, bf16[256,1536]{1,0:T(8,128)(2,1)}, f32[8,1536]{1,0:T(8,128)}, bf16[2,4,192,1152]{3,2,1,0:T(8,128)(2,1)}, bf16[4,192,384]{2,1,0:T(8,128)(2,1)}) custom-call(f32[256,1536]{1,0:T(8,128)} %get-tuple-element.65.x1_ref, f32[1536]{0:T(1024)} %gain_1d.4, bf16[256,1536]{1,0:T(8,128)(2,1)} %cot_ref.1, ...), custom_call_target="tpu_custom_call" | custom-call | tf_op jit(solution)/shard_map/feed_forward/pallas_call | solution.py:1205
  244.9 128.5 %recurrence_backward.1 = (bf16[256,1536]{1,0:T(8,128)(2,1)}, f32[16,128]{1,0:T(8,128)}, f32[4,8,512]{2,1,0:T(8,128)}, f32[16,128]{1,0:T(8,128)}, bf16[2,192,512]...) custom-call(bf16[256,1536]{1,0:T(8,128)(2,1)} %x_ref.3, ...), custom_call_target="tpu_custom_call" | custom-call | tf_op jit(solution)/shard_map/recurrence_backward/pallas_call | solution.py:1205
  373.4 5.2 %finish.1 = (f32[192,512]{1,0:T(8,128)}, f32[192,512]{1,0:T(8,128)}, f32[192,512]{1,0:T(8,128)}, f32[192,1152]{1,0:T(8,128)}, f32[192,1152]{1,0:T(8,128)}, /*ind...) custom-call(bf16[2,192,512]{2,1,0:T(8,128)(2,1)} %get-tuple-element., ...), custom_call_target="tpu_custom_call" | custom-call | tf_op jit(solution)/shard_map/finish/pallas_call | solution.py:1991

commit v3 on v2

--- a/solution.py
+++ b/solution.py
@@ -499,14 +499,15 @@
 
             def take(v, s):
                 self.w.landed(v(b, p.c), s[f"{left}{k - 1}"])
+                if k < 4:
+
+                    @pl.when(z < 3 if sign > 0 else z > 0)
+                    def _():
+                        self._start(v, b, s[f"{left}{k}"], p.line(z + sign))
+
                 self._start(v, b, s[f"o{left}{k - 1}"], p.partner())
 
             self._each(b, take, exists)
-            if k < 4:
-                more = z < 3 if sign > 0 else z > 0
-                self._each(
-                    b, lambda v, s: self._start(v, b, s[f"{left}{k}"], p.line(z + sign)), exists, more
-                )
 
     def finish(self):
         p = self.w.place
@@ -1593,13 +1594,12 @@
             gather.forward()
             units[0].step(3)
 
+
         @pl.when(k == 3)
         def _():
             gather.finish()
             down.start()
             down_odd.start()
-            units[0].step(4)
-            units[1].step(2)
 
         j = p.member(k)
         scan_rows(j)
@@ -1609,7 +1609,8 @@
             def _():
                 w.copy(tail.at[j], sums.at[z, j], tail_slots + 3 * k + away - 1, p.line(z - away)).start()
 
-    units[1].step(3)
+    units[0].step(4)
+    units[1].step(2)
     for made in later:
         made.wait()
 
@@ -1623,6 +1624,7 @@
 
     core_o = CoreSum(w, lambda q: gout.at[:, q], cbo)
     core_o.start()
+    units[1].step(3)
 
     def in_grad(m, right):
         @pl.loop(0, 4)
@@ -1632,6 +1634,8 @@
     in_grad(1, dzy)
     core_y = CoreSum(w, lambda q: gin.at[1, :, q], cbi.at[1])
     core_y.start()
+    core_o.finish()
+    line_o.first()
     def through(j, carry):
         after = zero
         for src in (3, 2, 1):
@@ -1760,10 +1764,6 @@
 
     @pl.loop(0, 5)
     def _(k):
-        @pl.when(k == 1)
-        def _():
-            units[1].step(4)
-            units[2].step(2)
 
         @pl.when(k == 4)
         def _():
@@ -1797,10 +1797,10 @@
 
         @pl.when(k == 0)
         def _():
-            core_o.finish()
-            line_o.first()
             core_y.finish()
             line_y.first()
+            units[1].step(4)
+            units[2].step(2)
 
         @pl.when(k == 1)
         def _():
@@ -1810,8 +1810,6 @@
         @pl.when(k == 2)
         def _():
             units[2].step(4)
-            spreads[0].start()
-            odds[0].start()
             line_o.step(2)
 
         @pl.when(k == 3)
@@ -1821,11 +1819,15 @@
             summed.to_x()
             line_o.step(3)
 
-    line_o.step(4)
+        @pl.when(k == 4)
+        def _():
+            line_o.step(4)
+            line_y.step(2)
+
     in_grad(0, oo)
     core_x.start()
     core_g.start()
-    line_y.step(2)
+    line_y.step(3)
     acc8[5:6, :] = jnp.sum(acc[0], axis=0, keepdims=True)
     acc8[6:7, :] = jnp.sum(acc[1], axis=0, keepdims=True)
     acc8[7:8, :] = -8.0 * sm_ref[8:9, :] * jnp.sum(acc[2], axis=0, keepdims=True)
@@ -1835,12 +1837,13 @@
     core_x.finish()
     core_g.finish()
     line_x.first()
-    line_y.step(3)
     line_y.step(4)
+    small_early.core()
+    summed.finish()
+    spreads[0].start()
+    odds[0].start()
     spreads[1].start()
     line_x.step(2)
-    small_early.core()
-    summed.finish()
 
     def last(i, carry):
         at = rows16(i)

time: 382 us -> 374 us (0.979)
  Pallas kernels: 378 us -> 371 us
    pallas_call x3, Pallas kernels: 373 us -> 365 us  [call(): pl.pallas_call(kernel, out_shape=outs, in_specs=[kinds[k] for k in spaces...]
where the time goes in v3:
time: 374 us; the launch traced here: 371 us
  Pallas kernels  371 us (99%)
    pallas_call x3, Pallas kernels, call(): pl.pallas_call(kernel, out_shape=outs, in_specs=[kinds[k] for k in spaces...  365 us

profile of v3, /device:TPU:4, one launch (start us, length us, event | category | flops | bytes accessed | tf_op | source)
XLA Modules:
  0.0 371.4 jit_solution(1656972729313806705)
XLA Ops:
  0.7 126.1 %recurrence_forward.1 = (f32[256,1536]{1,0:T(8,128)}, f32[8,1536]{1,0:T(8,128)}, f32[16,512]{1,0:T(8,128)}, bf16[1536,1024]{1,0:T(8,128)(2,1)}, bf16[2,4,2,192,5...) custom-call(bf16[256,1536]{1,0:T(8,128)(2,1)} %x_ref.3, ...), custom_call_target="tpu_custom_call" | custom-call | tf_op jit(solution)/shard_map/recurrence_forward/pallas_call | solution.py:1206
  126.8 113.4 %feed_forward.1 = (f32[256,1536]{1,0:T(8,128)}, bf16[256,1536]{1,0:T(8,128)(2,1)}, f32[8,1536]{1,0:T(8,128)}, bf16[2,4,192,1152]{3,2,1,0:T(8,128)(2,1)}, bf16[4,192,384]{2,1,0:T(8,128)(2,1)}) custom-call(f32[256,1536]{1,0:T(8,128)} %get-tuple-element.65.x1_ref, f32[1536]{0:T(1024)} %gain_1d.4, bf16[256,1536]{1,0:T(8,128)(2,1)} %cot_ref.1, ...), custom_call_target="tpu_custom_call" | custom-call | tf_op jit(solution)/shard_map/feed_forward/pallas_call | solution.py:1206
  240.2 125.8 %recurrence_backward.1 = (bf16[256,1536]{1,0:T(8,128)(2,1)}, f32[16,128]{1,0:T(8,128)}, f32[4,8,512]{2,1,0:T(8,128)}, f32[16,128]{1,0:T(8,128)}, bf16[2,192,512]...) custom-call(bf16[256,1536]{1,0:T(8,128)(2,1)} %x_ref.3, ...), custom_call_target="tpu_custom_call" | custom-call | tf_op jit(solution)/shard_map/recurrence_backward/pallas_call | solution.py:1206
  366.0 5.2 %finish.1 = (f32[192,512]{1,0:T(8,128)}, f32[192,512]{1,0:T(8,128)}, f32[192,512]{1,0:T(8,128)}, f32[192,1152]{1,0:T(8,128)}, f32[192,1152]{1,0:T(8,128)}, /*ind...) custom-call(bf16[2,192,512]{2,1,0:T(8,128)(2,1)} %get-tuple-element., ...), custom_call_target="tpu_custom_call" | custom-call | tf_op jit(solution)/shard_map/finish/pallas_call | solution.py:1994

commit v4 on v3

--- a/solution.py
+++ b/solution.py
@@ -1096,10 +1096,11 @@
         def _():
             line_g.step(3)
             line_u.step(2)
-
-        @pl.when(k == 3)
-        def _():
             gather_cot.forward()
+
+        @pl.when(k == 4)
+        def _():
+            line_u.step(3)
 
         @pl.when(k > 0)
         def _():
@@ -1132,7 +1133,6 @@
         aa[:, 256:264, :] = jnp.zeros((4, 8, 512), f32)
 
     line_g.step(4)
-    line_u.step(3)
 
     @pl.when(z < 3)
     def _():

time: 374 us -> 370 us (0.989)
  Pallas kernels: 371 us -> 367 us
where the time goes in v4:
time: 370 us; the launch traced here: 368 us
  Pallas kernels  367 us (99%)
    pallas_call x3, Pallas kernels, call(): pl.pallas_call(kernel, out_shape=outs, in_specs=[kinds[k] for k in spaces...  362 us

profile of v4, /device:TPU:4, one launch (start us, length us, event | category | flops | bytes accessed | tf_op | source)
XLA Modules:
  0.0 368.2 jit_solution(5430662361203406324)
XLA Ops:
  0.7 123.0 %recurrence_forward.1 = (f32[256,1536]{1,0:T(8,128)}, f32[8,1536]{1,0:T(8,128)}, f32[16,512]{1,0:T(8,128)}, bf16[1536,1024]{1,0:T(8,128)(2,1)}, bf16[2,4,2,192,5...) custom-call(bf16[256,1536]{1,0:T(8,128)(2,1)} %x_ref.3, ...), custom_call_target="tpu_custom_call" | custom-call | tf_op jit(solution)/shard_map/recurrence_forward/pallas_call | solution.py:1206
  123.6 113.4 %feed_forward.1 = (f32[256,1536]{1,0:T(8,128)}, bf16[256,1536]{1,0:T(8,128)(2,1)}, f32[8,1536]{1,0:T(8,128)}, bf16[2,4,192,1152]{3,2,1,0:T(8,128)(2,1)}, bf16[4,192,384]{2,1,0:T(8,128)(2,1)}) custom-call(f32[256,1536]{1,0:T(8,128)} %get-tuple-element.65.x1_ref, f32[1536]{0:T(1024)} %gain_1d.4, bf16[256,1536]{1,0:T(8,128)(2,1)} %cot_ref.1, ...), custom_call_target="tpu_custom_call" | custom-call | tf_op jit(solution)/shard_map/feed_forward/pallas_call | solution.py:1206
  237.0 125.8 %recurrence_backward.1 = (bf16[256,1536]{1,0:T(8,128)(2,1)}, f32[16,128]{1,0:T(8,128)}, f32[4,8,512]{2,1,0:T(8,128)}, f32[16,128]{1,0:T(8,128)}, bf16[2,192,512]...) custom-call(bf16[256,1536]{1,0:T(8,128)(2,1)} %x_ref.3, ...), custom_call_target="tpu_custom_call" | custom-call | tf_op jit(solution)/shard_map/recurrence_backward/pallas_call | solution.py:1206
  362.8 5.2 %finish.1 = (f32[192,512]{1,0:T(8,128)}, f32[192,512]{1,0:T(8,128)}, f32[192,512]{1,0:T(8,128)}, f32[192,1152]{1,0:T(8,128)}, f32[192,1152]{1,0:T(8,128)}, /*ind...) custom-call(bf16[2,192,512]{2,1,0:T(8,128)(2,1)} %get-tuple-element., ...), custom_call_target="tpu_custom_call" | custom-call | tf_op jit(solution)/shard_map/finish/pallas_call | solution.py:1994
